TPU v7x, 768 devices: a whole 4x8x12 slice. The times are simulated.
768 devices in a mesh: row: 192 (over y, z, core), col: 4 (over x).
Axes of the slice: x: 4, y: 8, z: 12, core: 2. Of those that a mesh axis runs over, the one named last changes fastest.
Arguments:
- matrix: bfloat16 [49152, 24576], P('row', 'col'), may hold values from 7 to 180000
- left_t: float32 [32, 49152], P(None, 'row'), may hold values from 0.5 to 2
- right: float32 [32, 24576], P(None, 'col'), may hold values from 0.5 to 2
Outputs:
- new_left_t: float32 [32, 49152], P(None, 'row')
- new_right: float32 [32, 24576], P(None, 'col')
All inputs are finite; a program needn't handle non-finite values.
Results may differ from a plain program's by a relative error of at most 0.0003.
Values sent between devices are 32-bit elements; how exact they have to be, the bound alone decides.
No kernel may reach another device: no remote copies, remote signals or barrier semaphores. Data moves between devices by JAX's collectives and lax.ppermute only.
A program may use at most 32 MiB of HBM per device.

v0:
```python
import jax
import jax.numpy as jnp
from jax import lax
from jax.sharding import PartitionSpec as P

HIGH = lax.Precision.HIGHEST


def local(matrix, left_t, right):
    tile_values = matrix.astype(jnp.float32)
    product = lax.dot_general(
        left_t, right, (((0,), (0,)), ((), ())), precision=HIGH, preferred_element_type=jnp.float32
    )
    quotient = tile_values / product
    numerator_part = lax.dot_general(
        right,
        quotient,
        (((1,), (1,)), ((), ())),
        precision=HIGH,
        preferred_element_type=jnp.float32,
    )
    numerator, right_mass = lax.psum((numerator_part, jnp.sum(right, axis=1)), "col")
    new_left_t = left_t * numerator / right_mass[:, None]
    product_two = lax.dot_general(
        new_left_t,
        right,
        (((0,), (0,)), ((), ())),
        precision=HIGH,
        preferred_element_type=jnp.float32,
    )
    quotient_two = tile_values / product_two
    partial_sums = jnp.dot(
        new_left_t, quotient_two, precision=HIGH, preferred_element_type=jnp.float32
    )
    local_mass = jnp.sum(new_left_t, axis=1)
    totals, left_mass = lax.psum((partial_sums, local_mass), "row")
    new_right = right * totals / left_mass[:, None]
    return (new_left_t, new_right)


def solution(mesh):
    placed = (P("row", "col"), P(None, "row"), P(None, "col"))
    return jax.shard_map(
        local,
        mesh=mesh,
        in_specs=placed,
        out_specs=(P(None, "row"), P(None, "col")),
        check_vma=False,
    )
```

profile of v0, /device:TPU:1, one launch (start us, length us, event | category | flops | bytes accessed | tf_op | source)
XLA Modules:
  0.0 441.2 jit_solution(13322064476685009872)
XLA Ops:
  7.2 0.0 all-reduce.3.cloned.1.call-start
  7.2 1.3 reduce_sum.18
  8.5 0.0 copy-start
  8.5 7.6 %convert_divide_fusion.1 = f32[256,6144]{1,0:T(8,128)S(1)} fusion(bf16[256,6144]{1,0:T(8,128)(2,1)} %param.3, f32[32,256]{1,0:T(8,128)} %param.4, f32[32,6144]{1,0:T(8,128)} %param.5), kind=kOutput, calls=%fused_computation.1 | convolution fusion | flops 607125504 | bytes 10256384 | tf_op jit(solution)/shard_map/dot_general | solution.py:11
  16.1 0.0 copy-done
  16.1 0.0 copy-start.2
  16.2 5.5 %convolution_bitcast_fusion = f32[32,256]{1,0:T(8,128)S(1)} fusion(f32[256,6144]{1,0:T(8,128)S(1)} %convert_divide_fusion.1, f32[32,6144]{1,0:T(8,128)S(1)} %copy-done), kind=kOutput, calls=%fused_computation.2 | convolution fusion | flops 603979776 | bytes 7110656 | tf_op jit(solution)/shard_map/dot_general | solution.py:15
  21.6 14.4 %all-reduce = (f32[32,256]{1,0:T(8,128)S(1)}, f32[32]{0:T(128)S(1)}) all-reduce(f32[32,256]{1,0:T(8,128)S(1)} %convolution_bitcast_fusion, f32[32]{0:T(128)S(1)} %reduce_sum.18), channel_id=1, replica_groups=mesh['row'=192,'col'=4] {'col'}, use_global_device_ids=true, to_apply=%region_0.0 | all-reduce | flops 8224 | bytes 65792 | tf_op jit(solution)/shard_map/psum | solution.py:22
  36.0 0.0 copy-done.2
  36.1 0.2 fusion
  36.2 0.0 copy-start.1
  36.3 7.3 %convert_divide_fusion = f32[256,6144]{1,0:T(8,128)S(1)} fusion(bf16[256,6144]{1,0:T(8,128)(2,1)} %param.3, f32[32,256]{1,0:T(8,128)S(1)} %get-tuple-element.5, f32[32,6144]{1,0:T(8,128)S(1)} %copy-done), kind=kOutput, calls=%fused_computation | convolution fusion | flops 607125504 | bytes 10256384 | tf_op jit(solution)/shard_map/dot_general | solution.py:24
  43.6 0.0 copy-done.1
  43.6 4.6 %fusion.1 = f32[32,6144]{1,0:T(8,128)} fusion(f32[32,256]{1,0:T(8,128)S(1)} %get-tuple-element.5, f32[256,6144]{1,0:T(8,128)S(1)} %convert_divide_fusion), kind=kOutput, calls=%fused_computation.6 | convolution fusion | flops 603979776 | bytes 7110656 | tf_op jit(solution)/shard_map/dot_general | solution.py:32
  48.1 0.0 all-reduce.3.cloned.1.call-update
  48.1 384.1 %psum.31 = f32[32]{0:T(128)S(1)} all-reduce(f32[32]{0:T(128)S(1)} %get-tuple-element.4), channel_id=1, replica_groups=mesh['row'=192,'col'=4] {'row'}, use_global_device_ids=true, to_apply=%region_5.0 | all-reduce | flops 32 | bytes 256 | tf_op jit(solution)/shard_map/psum | solution.py:36
  432.2 0.0 all-reduce.3.cloned.1.call-done
  432.2 2.1 multiply_divide_fusion
Async XLA Ops:
  7.2 425.1 %all-reduce.3.cloned.1.call-start = ((), (), s32[]{:S(2)}) async-start(), calls=%async_computation | async-start | bytes 1572864 | tf_op jit(solution)/shard_map/psum | solution.py:36
  8.5 7.6 %copy-start = (f32[32,6144]{1,0:T(8,128)S(1)}, f32[32,6144]{1,0:T(8,128)}, u32[]{:S(2)}) copy-start(f32[32,6144]{1,0:T(8,128)} %param.5) | copy-start | bytes 2359300
  16.1 19.9 %copy-start.2 = (f32[32,256]{1,0:T(8,128)S(1)}, f32[32,256]{1,0:T(8,128)}, u32[]{:S(2)}) copy-start(f32[32,256]{1,0:T(8,128)} %param.4) | copy-start | bytes 98308
  36.2 7.3 %copy-start.1 = (f32[32,256]{1,0:T(8,128)}, f32[32,256]{1,0:T(8,128)S(1)}, u32[]{:S(2)}) copy-start(f32[32,256]{1,0:T(8,128)S(1)} %get-tuple-element.5) | copy-start | bytes 98308
Sparse Core Ops, SparseCore 0:
  48.3 307.8 all-reduce.2
where the time goes:
time: 441 us
  blocking collectives  398 us (90%)
  matrix products  24.9 us (6%)
  between operations  14.1 us (3%)
    psum x1, blocking collectives, local(): totals, left_mass = lax.psum((partial_sums, local_mass), 'row')  384 us
    psum x1, blocking collectives, local(): lax.psum((numerator_part, jnp.sum(right, axis=1)), 'col')  14.4 us
  transfers between devices with their start and end apart: 1, of which 0 were waited for; matrix products, arithmetic and copies ran while one was open for 0% of the time, Pallas kernels for 0%

commit v1 on v0

v1 whole, which is shorter than its diff:
```python
import jax
import jax.numpy as jnp
from jax import lax
from jax.sharding import Mesh, PartitionSpec as P

HIGH = lax.Precision.HIGHEST
PLANE = ("y", "z")
SUB, LANE = 8, 128


def local(matrix, left_t, right):
    rank, rows = left_t.shape
    cols = right.shape[1]
    n_col = lax.axis_size("x")
    n_plane = lax.axis_size(PLANE)
    core = lax.axis_index("c")
    pair = [(0, 1), (1, 0)]
    tile_values = matrix.astype(jnp.float32)

    product = lax.dot_general(
        left_t, right, (((0,), (0,)), ((), ())), precision=HIGH, preferred_element_type=jnp.float32
    )
    quotient = tile_values / product
    part = lax.dot_general(
        right, quotient, (((1,), (1,)), ((), ())), precision=HIGH, preferred_element_type=jnp.float32
    )
    mass_part = jnp.broadcast_to(jnp.sum(right, axis=1)[:, None], (rank, LANE))
    sent = jnp.concatenate([part, mass_part], axis=1)
    sent = jnp.broadcast_to(sent[None], (n_col, *sent.shape))
    got = jnp.sum(lax.all_to_all(sent, "x", 0, 0), axis=0)
    new_left_t = left_t * got[:, :rows] / got[:, rows : rows + 1]

    product_two = lax.dot_general(
        new_left_t, right, (((0,), (0,)), ((), ())), precision=HIGH, preferred_element_type=jnp.float32
    )
    quotient_two = tile_values / product_two
    totals = jnp.dot(new_left_t, quotient_two, precision=HIGH, preferred_element_type=jnp.float32)
    mass = jnp.sum(new_left_t, axis=1)

    bands, strips = rank // SUB, cols // LANE
    n_tiles = bands * strips
    half = n_tiles // 2
    each = half // n_plane
    tiles = totals.reshape(bands, SUB, strips, LANE).transpose(0, 2, 1, 3).reshape(n_tiles, SUB, LANE)
    mass_tiles = jnp.broadcast_to(mass.reshape(bands, SUB)[:, :, None], (bands, SUB, LANE))
    own = lax.dynamic_slice_in_dim(tiles, core * half, half, 0)
    other = lax.dynamic_slice_in_dim(tiles, (1 - core) * half, half, 0)
    own_mass = lax.dynamic_slice_in_dim(mass_tiles, core * bands // 2, bands // 2, 0)
    other_mass = lax.dynamic_slice_in_dim(mass_tiles, (1 - core) * bands // 2, bands // 2, 0)
    there = lax.ppermute(jnp.concatenate([other, other_mass], axis=0), "c", pair)
    summed = own + there[:half]
    summed_mass = own_mass + there[half:]
    per_band = n_plane // (bands // 2)
    mass_of = jnp.repeat(summed_mass, per_band, axis=0)
    message = jnp.concatenate([summed.reshape(n_plane, each * SUB, LANE), mass_of], axis=1)
    arrived = jnp.sum(lax.all_to_all(message, PLANE, 0, 0), axis=0)
    done = arrived[: each * SUB].reshape(each, SUB, LANE) / arrived[None, each * SUB :]
    spread = jnp.broadcast_to(done[None], (n_plane, each, SUB, LANE))
    mine = lax.all_to_all(spread, PLANE, 0, 0).reshape(half, SUB, LANE)
    theirs = lax.ppermute(mine, "c", pair)
    low = jnp.where(core == 0, mine, theirs)
    high = jnp.where(core == 0, theirs, mine)
    whole = jnp.concatenate([low, high], axis=0)
    whole = whole.reshape(bands, strips, SUB, LANE).transpose(0, 2, 1, 3).reshape(rank, cols)
    return new_left_t, right * whole


def factor(mesh):
    n_row, n_col = mesh.shape["row"], mesh.shape["col"]
    n_z = 12 if n_row % 24 == 0 else 2
    shape = (n_row // (2 * n_z), n_z, 2, n_col)
    return Mesh(mesh.devices.reshape(shape), ("y", "z", "c", "x"))


def solution(mesh):
    row = ("y", "z", "c")
    return jax.shard_map(
        local,
        mesh=factor(mesh),
        in_specs=(P(row, "x"), P(None, row), P(None, "x")),
        out_specs=(P(None, row), P(None, "x")),
        check_vma=False,
    )
```

time: 441 us -> 133 us (0.30)
  blocking collectives: 398 us -> 73.1 us
  starting transfers between devices: 0.04 us -> 23.7 us
  between operations: 14.1 us -> 0.8 us
  waiting for transfers between devices: 0.02 us -> 7.84 us
    psum x2 -> x0, blocking collectives: 398 us -> none  [the longest x1 384 us: local(): totals, left_mass = lax.psum((partial_sums, local_mass), 'row')]
    all_to_all x0 -> x2, blocking collectives: none -> 73.1 us  [the longest x1 45.5 us: local(): arrived = jnp.sum(lax.all_to_all(message, PLANE, 0, 0), axis=0)]
    ppermute x0 -> x2, starting transfers between devices: none -> 18.9 us  [the longest x1 12 us: local(): lax.ppermute(jnp.concatenate([other, other_mass], axis=0), 'c', pair)]
    all_to_all x0 -> x1, waiting for transfers between devices: none -> 5.18 us  [local(): got = jnp.sum(lax.all_to_all(sent, 'x', 0, 0), axis=0)]
    all_to_all x0 -> x1, starting transfers between devices: none -> 4.83 us  [local(): got = jnp.sum(lax.all_to_all(sent, 'x', 0, 0), axis=0)]
  transfers between devices with their start and end apart: 1 -> 3, of which waited for: 0 -> 3; matrix products, arithmetic and copies ran while one was open for 0% -> 0% of each run, Pallas kernels for 0% -> 0%
where the time goes in v1:
time: 133 us; the launch traced here: 132 us
  blocking collectives  73.1 us (55%)
  matrix products  24 us (18%)
  starting transfers between devices  23.7 us (18%)
  waiting for transfers between devices  7.84 us (6%)
  other arithmetic  1.75 us (1%)
    all_to_all x1, blocking collectives, local(): arrived = jnp.sum(lax.all_to_all(message, PLANE, 0, 0), axis=0)  45.5 us
    all_to_all x1, blocking collectives, local(): mine = lax.all_to_all(spread, PLANE, 0, 0).reshape(half, SUB, LANE)  27.6 us
    ppermute x1, starting transfers between devices, local(): lax.ppermute(jnp.concatenate([other, other_mass], axis=0), 'c', pair)  12 us
    dot_general x1, matrix products, local(): lax.dot_general(left_t, right, (((0,), (0,)), ((), ())), precision=HIGH,...  7.6 us
    dot_general x1, matrix products, local(): lax.dot_general(new_left_t, right, (((0,), (0,)), ((), ())), precision=HI...  7.27 us
    ppermute x1, starting transfers between devices, local(): theirs = lax.ppermute(mine, 'c', pair)  6.85 us
    dot_general x1, matrix products, local(): lax.dot_general(right, quotient, (((1,), (1,)), ((), ())), precision=HIGH...  5.46 us
    all_to_all x1, waiting for transfers between devices, local(): got = jnp.sum(lax.all_to_all(sent, 'x', 0, 0), axis=0)  5.18 us
  transfers between devices with their start and end apart: 3, of which 3 were waited for; matrix products, arithmetic and copies ran while one was open for 0% of the time, Pallas kernels for 0%

profile of v1, /device:TPU:1, one launch (start us, length us, event | category | flops | bytes accessed | tf_op | source)
XLA Modules:
  0.0 132.4 jit_solution(11792659552730689014)
XLA Ops:
  0.6 0.0 copy-start
  0.6 7.6 %convert_divide_fusion.1 = f32[256,6144]{1,0:T(8,128)S(1)} fusion(bf16[256,6144]{1,0:T(8,128)(2,1)} %param.3, f32[32,256]{1,0:T(8,128)} %param.4, f32[32,6144]{1,0:T(8,128)} %param.5), kind=kOutput, calls=%fused_computation.1 | convolution fusion | flops 607125504 | bytes 10256384 | tf_op jit(solution)/shard_map/dot_general | solution.py:20
  8.2 0.0 copy-done
  8.3 0.0 copy-start.2
  8.3 5.5 %convolution_bitcast_fusion = f32[32,256]{1,0:T(8,128)S(1)} fusion(f32[256,6144]{1,0:T(8,128)S(1)} %convert_divide_fusion.1, f32[32,6144]{1,0:T(8,128)S(1)} %copy-done), kind=kOutput, calls=%fused_computation.2 | convolution fusion | flops 603979776 | bytes 7110656 | tf_op jit(solution)/shard_map/dot_general | solution.py:24
  13.7 0.2 reduce_sum.36
  13.9 0.1 broadcast_in_dim.14
  14.0 0.7 broadcast_in_dim.15
  14.7 4.8 %all-to-all-start = ((f32[4,32,384]{2,1,0:T(8,128)}), f32[4,32,384]{2,1,0:T(8,128)S(1)}, u32[]{:S(2)}, u32[]{:S(2)}) async-start(f32[4,32,384]{2,1,0:T(8,128)} %broadcast_in_dim.15), calls=%async_computation | async-start | bytes 393216 | tf_op jit(solution)/shard_map/all_to_all | solution.py:30
  19.5 5.2 %all-to-all-done = f32[4,32,384]{2,1,0:T(8,128)S(1)} async-done(((f32[4,32,384]{2,1,0:T(8,128)}), f32[4,32,384]{2,1,0:T(8,128)S(1)}, u32[]{:S(2)}, u32[]{:S(2)}) %all-to-all-start) | async-done | bytes 196640 | tf_op jit(solution)/shard_map/all_to_all | solution.py:30
  24.7 0.1 slice_reduce_fusion
  24.8 0.0 copy-done.2
  24.8 0.2 fusion.1
  25.0 0.0 copy-start.1
  25.0 0.1 broadcast_in_dim.16
  25.1 7.3 %convert_divide_fusion = f32[256,6144]{1,0:T(8,128)S(1)} fusion(bf16[256,6144]{1,0:T(8,128)(2,1)} %param.3, f32[32,256]{1,0:T(8,128)S(1)} %get-tuple-element.3, f32[32,6144]{1,0:T(8,128)S(1)} %copy-done), kind=kOutput, calls=%fused_computation | convolution fusion | flops 607125504 | bytes 10256384 | tf_op jit(solution)/shard_map/dot_general | solution.py:33
  32.4 0.0 copy-done.1
  32.4 3.7 %fusion.3 = f32[32,6144]{1,0:T(8,128)S(1)} fusion(f32[32,256]{1,0:T(8,128)S(1)} %get-tuple-element.3, f32[256,6144]{1,0:T(8,128)S(1)} %convert_divide_fusion), kind=kOutput, calls=%fused_computation.19 | convolution fusion | flops 603979776 | bytes 7110656 | tf_op jit(solution)/shard_map/dot_general | solution.py:37
  36.1 0.1 broadcast_in_dim.34
  36.2 12.0 %collective-permute-start = (f32[98,8,128]{2,1,0:T(8,128)S(1)}, f32[98,8,128]{2,1,0:T(8,128)S(1)}, u32[]{:S(2)}, u32[]{:S(2)}) collective-permute-start(f32[98,8,128]{2,1,0:T(8,128)S(1)} %pad_maximum_fusion.2), channel_id=1, source_target_pairs={{0,4},{4,0},{1,5},{5,1},{2,6},{6,2},{3,7},{7,3},{8,12},{12,8},{9,1... | collective-permute-start | bytes 1204232 | tf_op jit(solution)/shard_map/ppermute | solution.py:50
  48.3 1.3 %collective-permute-done = f32[98,8,128]{2,1,0:T(8,128)S(1)} collective-permute-done((f32[98,8,128]{2,1,0:T(8,128)S(1)}, f32[98,8,128]{2,1,0:T(8,128)S(1)}, u32[]{:S(2)}, u32[]{:S(2)}) %collective-permute-start) | collective-permute-done | bytes 401440 | tf_op jit(solution)/shard_map/ppermute | solution.py:50
  49.7 0.1 slice_add_fusion.1
  49.8 0.1 pad_maximum_fusion
  49.8 45.5 %all_to_all.15 = f32[96,16,128]{2,1,0:T(8,128)S(1)} all-to-all(f32[96,16,128]{2,1,0:T(8,128)S(1)} %pad_maximum_fusion), channel_id=1, replica_groups=mesh['y'=8,'z'=12,'c'=2,'x'=4] {'y','z'}, dimensions={0} | all-to-all | bytes 1572864 | tf_op jit(solution)/shard_map/all_to_all | solution.py:56
  95.3 0.1 reduce_sum.39
  95.5 27.6 %all_to_all.16 = f32[96,1,8,128]{3,2,1,0:T(8,128)S(1)} all-to-all(f32[96,1,8,128]{3,2,1,0:T(8,128)S(1)} %broadcast_in_dim.37), channel_id=1, replica_groups=mesh['y'=8,'z'=12,'c'=2,'x'=4] {'y','z'}, dimensions={0} | all-to-all | bytes 786432 | tf_op jit(solution)/shard_map/all_to_all | solution.py:59
  123.1 6.8 %collective-permute-start.1 = (f32[96,8,128]{2,1,0:T(8,128)S(1)}, f32[96,8,128]{2,1,0:T(8,128)S(1)}, u32[]{:S(2)}, u32[]{:S(2)}) collective-permute-start(f32[96,8,128]{2,1,0:T(8,128)S(1)} %bitcast.27), channel_id=1, source_target_pairs={{0,4},{4,0},{1,5},{5,1},{2,6},{6,2},{3,7},{7,3},{8,12},{12,8},{9,1... | collective-permute-start | bytes 1179656 | tf_op jit(solution)/shard_map/ppermute | solution.py:60
  130.0 1.3 collective-permute-done.1
  131.3 0.1 broadcast_select_fusion.1
  131.3 0.1 pad_maximum_fusion.1
  131.4 1.0 mul.23
  (9 shorter events, 0.2 us)
Async XLA Ops:
  0.6 7.6 %copy-start = (f32[32,6144]{1,0:T(8,128)S(1)}, f32[32,6144]{1,0:T(8,128)}, u32[]{:S(2)}) copy-start(f32[32,6144]{1,0:T(8,128)} %param.5) | copy-start | bytes 2359300
  8.3 16.6 %copy-start.2 = (f32[32,256]{1,0:T(8,128)S(1)}, f32[32,256]{1,0:T(8,128)}, u32[]{:S(2)}) copy-start(f32[32,256]{1,0:T(8,128)} %param.4) | copy-start | bytes 98308
  14.7 10.0 %all-to-all-start = ((f32[4,32,384]{2,1,0:T(8,128)}), f32[4,32,384]{2,1,0:T(8,128)S(1)}, u32[]{:S(2)}, u32[]{:S(2)}) async-start(f32[4,32,384]{2,1,0:T(8,128)} %broadcast_in_dim.15), calls=%async_computation | async-start | bytes 393216 | tf_op jit(solution)/shard_map/all_to_all | solution.py:30
  25.0 7.4 %copy-start.1 = (f32[32,256]{1,0:T(8,128)}, f32[32,256]{1,0:T(8,128)S(1)}, u32[]{:S(2)}) copy-start(f32[32,256]{1,0:T(8,128)S(1)} %get-tuple-element.3) | copy-start | bytes 98308
  36.2 13.4 %collective-permute-start = (f32[98,8,128]{2,1,0:T(8,128)S(1)}, f32[98,8,128]{2,1,0:T(8,128)S(1)}, u32[]{:S(2)}, u32[]{:S(2)}) collective-permute-start(f32[98,8,128]{2,1,0:T(8,128)S(1)} %pad_maximum_fusion.2), channel_id=1, source_target_pairs={{0,4},{4,0},{1,5},{5,1},{2,6},{6,2},{3,7},{7,3},{8,12},{12,8},{9,1... | collective-permute-start | bytes 1204232 | tf_op jit(solution)/shard_map/ppermute | solution.py:50
  123.1 8.2 %collective-permute-start.1 = (f32[96,8,128]{2,1,0:T(8,128)S(1)}, f32[96,8,128]{2,1,0:T(8,128)S(1)}, u32[]{:S(2)}, u32[]{:S(2)}) collective-permute-start(f32[96,8,128]{2,1,0:T(8,128)S(1)} %bitcast.27), channel_id=1, source_target_pairs={{0,4},{4,0},{1,5},{5,1},{2,6},{6,2},{3,7},{7,3},{8,12},{12,8},{9,1... | collective-permute-start | bytes 1179656 | tf_op jit(solution)/shard_map/ppermute | solution.py:60

commit v2 on v1

v2 whole, which is shorter than its diff:
```python
import functools

import jax
import jax.numpy as jnp
from jax import lax
from jax.experimental import pallas as pl
from jax.experimental.pallas import tpu as pltpu
from jax.sharding import Mesh, PartitionSpec as P

SUB, LANE = 8, 128
F32, BF16 = jnp.float32, jnp.bfloat16
NT = (((1,), (1,)), ((), ()))


def split(x):
    high = x.astype(BF16)
    return high, (x - high.astype(F32)).astype(BF16)


def dot(a, b):
    return jnp.dot(a, b, preferred_element_type=F32)


def stack_left(left):
    rank = left.shape[0]
    wide = jnp.concatenate([left] * 4, axis=0).T
    high = wide.astype(BF16).astype(F32)
    lane = lax.broadcasted_iota(jnp.int32, wide.shape, 1)
    return jnp.where(lane < 2 * rank, high, wide - high).astype(BF16)


def pack_column(column):
    bands = column.shape[0] // SUB
    lane = lax.broadcasted_iota(jnp.int32, (SUB, LANE), 1) // (LANE // bands)
    tile = jnp.zeros((SUB, LANE), F32)
    for b in range(bands):
        tile = jnp.where(lane == b, column[b * SUB : (b + 1) * SUB], tile)
    return tile


def unpack_column(tile, bands):
    lane = lax.broadcasted_iota(jnp.int32, (SUB, LANE), 1) // (LANE // bands)
    return [jnp.max(jnp.where(lane == b, tile, 0.0), axis=1, keepdims=True) for b in range(bands)]


def left_kernel(matrix_ref, left_ref, right_ref, out_ref, stacked, total, mass):
    step = pl.program_id(0)
    rank, rows = left_ref.shape

    @pl.when(step == 0)
    def _():
        stacked[...] = stack_left(left_ref[...])
        total[...] = jnp.zeros_like(total)
        mass[...] = jnp.zeros_like(mass)

    right = right_ref[...]
    high, low = split(right)
    product = dot(stacked[...], jnp.concatenate([high, low, high, low], axis=0))
    quotient = matrix_ref[...].astype(F32) / product
    q_high, q_low = split(quotient)
    both = lax.dot_general(
        jnp.concatenate([high, low], axis=0), q_high, NT, preferred_element_type=F32
    )
    rest = lax.dot_general(high, q_low, NT, preferred_element_type=F32)
    total[...] += both[:rank] + both[rank:] + rest
    mass[...] += sum(right[:, s : s + LANE] for s in range(0, right.shape[1], LANE))

    @pl.when(step == pl.num_programs(0) - 1)
    def _():
        bands, strips = rank // SUB, rows // LANE
        packed = pack_column(jnp.sum(mass[...], axis=1, keepdims=True))
        for peer in range(out_ref.shape[0]):
            for b in range(bands):
                for s in range(strips):
                    out_ref[peer, b * strips + s] = total[
                        b * SUB : (b + 1) * SUB, s * LANE : (s + 1) * LANE
                    ]
            out_ref[peer, bands * strips] = packed


def right_kernel(first, half_ref, matrix_ref, source_ref, left_ref, right_ref, *refs):
    del half_ref
    if first:
        out_ref, new_ref, stacked, pair = refs
    else:
        out_ref, stacked, pair = refs
    step = pl.program_id(0)
    rank, rows = left_ref.shape
    bands, strips = rank // SUB, rows // LANE
    n_out = out_ref.shape[0]

    @pl.when(step == 0)
    def _():
        if first:
            got = sum(source_ref[peer] for peer in range(source_ref.shape[0]))
            masses = unpack_column(got[bands * strips], bands)
            for b in range(bands):
                for s in range(strips):
                    at = (slice(b * SUB, (b + 1) * SUB), slice(s * LANE, (s + 1) * LANE))
                    new_ref[at] = left_ref[at] * got[b * strips + s] / masses[b]
            new = new_ref[...]
        else:
            new = left_ref[...]
        stacked[...] = stack_left(new)
        high, low = split(new)
        pair[...] = jnp.concatenate([high, low], axis=0)
        out_ref[n_out - 1] = pack_column(jnp.sum(new, axis=1, keepdims=True))

    high, low = split(right_ref[...])
    product = dot(stacked[...], jnp.concatenate([high, low, high, low], axis=0))
    quotient = matrix_ref[...].astype(F32) / product
    q_high, q_low = split(quotient)
    both = dot(pair[...], q_high)
    rest = dot(pair[:rank], q_low)
    total = both[:rank] + both[rank:] + rest
    wide = total.shape[1] // LANE
    per_band = (n_out - 1) // bands
    for b in range(bands):
        for s in range(wide):
            out_ref[b * per_band + step * wide + s] = total[
                b * SUB : (b + 1) * SUB, s * LANE : (s + 1) * LANE
            ]


def block_of(width):
    return 1024 if width % 1024 == 0 else LANE


def cost(rows, cols, rank):
    return pl.CostEstimate(
        flops=14 * rows * cols * rank, bytes_accessed=2 * rows * cols + 8 * rank * cols, transcendentals=rows * cols
    )


def left_phase(matrix, left_t, right, n_col):
    (rank, rows), cols = left_t.shape, right.shape[1]
    width = block_of(cols)
    n_tiles = rank * rows // (SUB * LANE) + 1
    return pl.pallas_call(
        left_kernel,
        name="left_phase",
        out_shape=jax.ShapeDtypeStruct((n_col, n_tiles, SUB, LANE), F32),
        grid=(cols // width,),
        in_specs=[
            pl.BlockSpec((rows, width), lambda i: (0, i)),
            pl.BlockSpec((rank, rows), lambda i: (0, 0)),
            pl.BlockSpec((rank, width), lambda i: (0, i)),
        ],
        out_specs=pl.BlockSpec((n_col, n_tiles, SUB, LANE), lambda i: (0, 0, 0, 0)),
        scratch_shapes=[
            pltpu.VMEM((rows, 4 * rank), BF16),
            pltpu.VMEM((rank, rows), F32),
            pltpu.VMEM((rank, LANE), F32),
        ],
        cost_estimate=cost(rows, cols, rank),
    )(matrix, left_t, right)


def right_phase(first, half, matrix, source, left_t, right):
    (rank, rows), cols = left_t.shape, right.shape[1] // 2
    width = block_of(cols)
    steps = cols // width
    n_tiles = rank * cols // (SUB * LANE) + 1
    whole = lambda shape: pl.BlockSpec(shape, lambda i, h: (0,) * len(shape))
    out_shape = [jax.ShapeDtypeStruct((n_tiles, SUB, LANE), F32)]
    out_specs = [whole((n_tiles, SUB, LANE))]
    if first:
        out_shape.append(jax.ShapeDtypeStruct((rank, rows), F32))
        out_specs.append(whole((rank, rows)))
    return pl.pallas_call(
        functools.partial(right_kernel, first),
        name="right_first" if first else "right_second",
        out_shape=out_shape,
        grid_spec=pltpu.PrefetchScalarGridSpec(
            num_scalar_prefetch=1,
            grid=(steps,),
            in_specs=[
                pl.BlockSpec((rows, width), lambda i, h: (0, h[0] * steps + i)),
                whole(source.shape),
                whole((rank, rows)),
                pl.BlockSpec((rank, width), lambda i, h: (0, h[0] * steps + i)),
            ],
            out_specs=out_specs,
            scratch_shapes=[pltpu.VMEM((rows, 4 * rank), BF16), pltpu.VMEM((2 * rank, rows), BF16)],
        ),
        cost_estimate=cost(rows, cols, rank),
    )(half, matrix, source, left_t, right)


def local(matrix, left_t, right):
    rank, cols = right.shape
    n_y, n_z, n_col = lax.axis_size("y"), lax.axis_size("z"), lax.axis_size("x")
    core = lax.axis_index("c")
    partner = [(0, 1), (1, 0)]

    sent = left_phase(matrix, left_t, right, n_col)
    got = lax.all_to_all(sent, "x", 0, 0)
    other = jnp.reshape(1 - core, (1,)).astype(jnp.int32)
    own = jnp.reshape(core, (1,)).astype(jnp.int32)
    for_partner, new_left_t = right_phase(True, other, matrix, got, left_t, right)
    there = lax.ppermute(for_partner, "c", partner)
    (here,) = right_phase(False, own, matrix, new_left_t, new_left_t, right)

    bands, strips = rank // SUB, cols // (2 * LANE)
    half = bands * strips
    summed = here + there
    masses = jnp.broadcast_to(summed[half:][None], (n_y, 1, SUB, LANE))
    message = jnp.concatenate([summed[:half].reshape(n_y, n_z, SUB, LANE), masses], axis=1)
    line = jnp.sum(lax.all_to_all(message, "y", 0, 0), axis=0)
    masses = jnp.broadcast_to(line[n_z:], (n_z, SUB, LANE))
    point = jnp.sum(lax.all_to_all(jnp.stack([line[:n_z], masses], axis=1), "z", 0, 0), axis=0)
    band = (lax.axis_index("y") * n_z + lax.axis_index("z")) // strips
    mass = lax.dynamic_slice(point[1], (0, band * (LANE // bands)), (SUB, 1))
    done = point[0] / mass
    line = lax.all_to_all(jnp.broadcast_to(done[None], (n_z, SUB, LANE)), "z", 0, 0)
    mine = lax.all_to_all(jnp.broadcast_to(line[None], (n_y, n_z, SUB, LANE)), "y", 0, 0)
    mine = mine.reshape(bands, strips, SUB, LANE)
    theirs = lax.ppermute(mine, "c", partner)
    low = jnp.where(core == 0, mine, theirs)
    high = jnp.where(core == 0, theirs, mine)
    whole = jnp.concatenate([low, high], axis=1).transpose(0, 2, 1, 3).reshape(rank, cols)
    return new_left_t, right * whole


def factor(mesh):
    n_row, n_col = mesh.shape["row"], mesh.shape["col"]
    n_z = 12 if n_row % 24 == 0 else 2
    shape = (n_row // (2 * n_z), n_z, 2, n_col)
    return Mesh(mesh.devices.reshape(shape), ("y", "z", "c", "x"))


def solution(mesh):
    row = ("y", "z", "c")
    return jax.shard_map(
        local,
        mesh=factor(mesh),
        in_specs=(P(row, "x"), P(None, row), P(None, "x")),
        out_specs=(P(None, row), P(None, "x")),
        check_vma=False,
    )
```

time: 133 us -> 116 us (0.87)
  blocking collectives: 73.1 us -> 45.2 us
  matrix products: 24 us -> 0 us
  Pallas kernels: 0 us -> 15.3 us
  starting transfers between devices: 23.7 us -> 33.9 us
  waiting for transfers between devices: 7.84 us -> 16.2 us
    all_to_all x2 -> x3, blocking collectives: 73.1 us -> 45.2 us  [the longest x1 18.4 us: local(): line = jnp.sum(lax.all_to_all(message, 'y', 0, 0), axis=0)]
    dot_general x4 -> x0, matrix products: 24 us -> none  [the longest x1 7.6 us: local(): lax.dot_general(left_t, right, (((0,), (0,)), ((), ())), precision=HIGH,...]
    pallas_call x0 -> x3, Pallas kernels: none -> 15.3 us  [the longest x2 8.37 us: right_phase(): pl.pallas_call(functools.partial(right_kernel, first), name='right_first'...]
    all_to_all x1 -> x2, starting transfers between devices: 4.83 us -> 15.9 us  [the longest x1 11.1 us: local(): lax.all_to_all(jnp.stack([line[:n_z], masses], axis=1), 'z', 0, 0)]
    all_to_all x1 -> x2, waiting for transfers between devices: 5.18 us -> 14.9 us  [the longest x1 10 us: local(): lax.all_to_all(jnp.stack([line[:n_z], masses], axis=1), 'z', 0, 0)]
    ppermute x2, waiting for transfers between devices: 2.66 us -> 1.33 us  [the longest x1 1.32 us: local(): theirs = lax.ppermute(mine, 'c', partner)]
  transfers between devices with their start and end apart: 3 -> 4, of which waited for: 3 -> 3; matrix products, arithmetic and copies ran while one was open for 0% -> 0% of each run, Pallas kernels for 0% -> 4%
where the time goes in v2:
time: 116 us; the launch traced here: 115 us
  blocking collectives  45.2 us (39%)
  starting transfers between devices  33.9 us (29%)
  waiting for transfers between devices  16.2 us (14%)
  Pallas kernels  15.3 us (13%)
  other arithmetic  2.85 us (2%)
    all_to_all x1, blocking collectives, local(): line = jnp.sum(lax.all_to_all(message, 'y', 0, 0), axis=0)  18.4 us
    all_to_all x1, blocking collectives, local(): lax.all_to_all(jnp.broadcast_to(line[None], (n_y, n_z, SUB, LANE)), 'y',...  13.9 us
    all_to_all x1, blocking collectives, local(): lax.all_to_all(jnp.broadcast_to(done[None], (n_z, SUB, LANE)), 'z', 0, 0)  13 us
    ppermute x1, starting transfers between devices, local(): there = lax.ppermute(for_partner, 'c', partner)  12 us
    all_to_all x1, starting transfers between devices, local(): lax.all_to_all(jnp.stack([line[:n_z], masses], axis=1), 'z', 0, 0)  11.1 us
    all_to_all x1, waiting for transfers between devices, local(): lax.all_to_all(jnp.stack([line[:n_z], masses], axis=1), 'z', 0, 0)  10 us
    pallas_call x2, Pallas kernels, right_phase(): pl.pallas_call(functools.partial(right_kernel, first), name='right_first'...  8.37 us
    pallas_call x1, Pallas kernels, left_phase(): pl.pallas_call(left_kernel, name='left_phase', out_shape=jax.ShapeDtypeSt...  6.94 us
  transfers between devices with their start and end apart: 4, of which 3 were waited for; matrix products, arithmetic and copies ran while one was open for 0% of the time, Pallas kernels for 4%

profile of v2, /device:TPU:1, one launch (start us, length us, event | category | flops | bytes accessed | tf_op | source)
XLA Modules:
  0.0 115.3 jit_solution(3875194289368381572)
XLA Ops:
  0.6 6.9 %left_phase.1 = f32[4,9,8,128]{3,2,1,0:T(8,128)} custom-call(bf16[256,6144]{1,0:T(8,128)(2,1)} %matrix_ref.5, f32[32,256]{1,0:T(8,128)} %left_ref.3, f32[32,6144]{1,0:T(8,128)} %right_ref.5), custom_call_target="tpu_custom_call" | custom-call | flops 704643072 | bytes 4718592 | tf_op jit(solution)/shard_map/left_phase/pallas_call | solution.py:139
  7.6 4.8 %all-to-all-start = ((f32[4,9,8,128]{3,2,1,0:T(8,128)}), f32[4,9,8,128]{3,2,1,0:T(8,128)S(1)}, u32[]{:S(2)}, u32[]{:S(2)}) async-start(f32[4,9,8,128]{3,2,1,0:T(8,128)} %left_phase.1), calls=%async_computation | async-start | bytes 294912 | tf_op jit(solution)/shard_map/all_to_all | solution.py:197
  12.4 4.9 %all-to-all-done.source_ref = f32[4,9,8,128]{3,2,1,0:T(8,128)S(1)} async-done(((f32[4,9,8,128]{3,2,1,0:T(8,128)}), f32[4,9,8,128]{3,2,1,0:T(8,128)S(1)}, u32[]{:S(2)}, u32[]{:S(2)}) %all-to-all-start) | async-done | bytes 147488 | tf_op jit(solution)/shard_map/all_to_all | solution.py:197
  17.3 0.0 copy-start.1
  17.3 0.6 copy-done.1
  18.0 4.2 %right_first.1 = (f32[97,8,128]{2,1,0:T(8,128)}, f32[32,256]{1,0:T(8,128)}) custom-call(s32[1]{0:T(128)} %bitcast.half_ref, bf16[256,6144]{1,0:T(8,128)(2,1)} %matrix_ref.5, f32[4,9,8,128]{3,2,1,0:T(8,128)} %copy-done.1, f32[32,256]{1,0:T(8,128)} %left_ref.3, f32[32,6144]{1,0:T(8,128)} %right_ref.5), custom_call_target="tpu_custom_call" | custom-call | flops 352321536 | bytes 2359296 | tf_op jit(solution)/shard_map/right_first/pallas_call | solution.py:170
  22.2 12.0 %collective-permute-start = (f32[97,8,128]{2,1,0:T(8,128)}, f32[97,8,128]{2,1,0:T(8,128)S(1)}, u32[]{:S(2)}, u32[]{:S(2)}) collective-permute-start(f32[97,8,128]{2,1,0:T(8,128)} %get-tuple-element.5), channel_id=1, source_target_pairs={{0,4},{4,0},{1,5},{5,1},{2,6},{6,2},{3,7},{7,3},{8,12},{12,8},{9,1... | collective-permute-start | bytes 1191944 | tf_op jit(solution)/shard_map/ppermute | solution.py:201
  34.2 4.1 %right_second.1 = f32[97,8,128]{2,1,0:T(8,128)} custom-call(s32[1]{0:T(128)} %bitcast.1.half_ref, bf16[256,6144]{1,0:T(8,128)(2,1)} %matrix_ref.5, f32[32,256]{1,0:T(8,128)} %get-tuple-element.2.source_ref.left_ref, f32[32,256]{1,0:T(8,128)} %get-tuple-element.2.source_ref.left_ref, f32[32,6144]{1,0:T(8,128)} %right_ref.5), custom_call_target="tpu_custom_call" | custom-call | flops 352321536 | bytes 2359296 | tf_op jit(solution)/shard_map/right_second/pallas_call | solution.py:170
  38.3 0.0 collective-permute-done
  38.3 1.0 add.10
  39.4 0.0 copy-start
  39.5 18.4 %all_to_all.25 = f32[8,13,8,128]{3,2,1,0:T(8,128)S(1)} all-to-all(f32[8,13,8,128]{3,2,1,0:T(8,128)S(1)} %pad_maximum_fusion), channel_id=1, replica_groups=mesh['y'=8,'z'=12,'c'=2,'x'=4] {'y'}, dimensions={0} | all-to-all | bytes 851968 | tf_op jit(solution)/shard_map/all_to_all | solution.py:209
  58.0 0.6 pad_maximum_fusion.1
  58.6 11.1 %all-to-all-start.2 = ((f32[12,2,8,128]{3,2,1,0:T(8,128)}), f32[12,2,8,128]{3,2,1,0:T(8,128)S(1)}, u32[]{:S(2)}, u32[]{:S(2)}) async-start(f32[12,2,8,128]{3,2,1,0:T(8,128)} %pad_maximum_fusion.1), calls=%async_computation.2 | async-start | bytes 196608 | tf_op jit(solution)/shard_map/all_to_all | solution.py:211
  69.7 10.0 %all-to-all-done.2 = f32[12,2,8,128]{3,2,1,0:T(8,128)S(1)} async-done(((f32[12,2,8,128]{3,2,1,0:T(8,128)}), f32[12,2,8,128]{3,2,1,0:T(8,128)S(1)}, u32[]{:S(2)}, u32[]{:S(2)}) %all-to-all-start.2) | async-done | bytes 98336 | tf_op jit(solution)/shard_map/all_to_all | solution.py:211
  79.8 0.2 dynamic-slice_reduce_fusion
  80.0 0.1 fusion.1
  80.1 13.0 %all_to_all.26 = f32[12,8,128]{2,1,0:T(8,128)S(1)} all-to-all(f32[12,8,128]{2,1,0:T(8,128)S(1)} %broadcast_in_dim.25), channel_id=1, replica_groups=mesh['y'=8,'z'=12,'c'=2,'x'=4] {'z'}, dimensions={0} | all-to-all | bytes 98304 | tf_op jit(solution)/shard_map/all_to_all | solution.py:215
  93.0 13.9 %all_to_all.27 = f32[8,12,8,128]{3,2,1,0:T(8,128)S(1)} all-to-all(f32[8,12,8,128]{3,2,1,0:T(8,128)S(1)} %broadcast_in_dim.26), channel_id=1, replica_groups=mesh['y'=8,'z'=12,'c'=2,'x'=4] {'y'}, dimensions={0} | all-to-all | bytes 786432 | tf_op jit(solution)/shard_map/all_to_all | solution.py:216
  106.9 6.0 %collective-permute-start.1 = (f32[4,24,8,128]{3,2,1,0:T(8,128)S(1)}, f32[4,24,8,128]{3,2,1,0:T(8,128)S(1)}, u32[]{:S(2)}, u32[]{:S(2)}) collective-permute-start(f32[4,24,8,128]{3,2,1,0:T(8,128)S(1)} %bitcast.21), channel_id=1, source_target_pairs={{0,4},{4,0},{1,5},{5,1},{2,6},{6,2},{3,7},{7,3},{8,12},{12,8},{9,1... | collective-permute-start | bytes 1179656 | tf_op jit(solution)/shard_map/ppermute | solution.py:218
  113.0 1.3 %collective-permute-done.1 = f32[4,24,8,128]{3,2,1,0:T(8,128)S(1)} collective-permute-done((f32[4,24,8,128]{3,2,1,0:T(8,128)S(1)}, f32[4,24,8,128]{3,2,1,0:T(8,128)S(1)}, u32[]{:S(2)}, u32[]{:S(2)}) %collective-permute-start.1) | collective-permute-done | bytes 393248 | tf_op jit(solution)/shard_map/ppermute | solution.py:218
  114.3 0.1 broadcast_select_fusion.1
  114.3 0.0 copy-done
  114.4 1.0 fusion
  (12 shorter events, 0.2 us)
Async XLA Ops:
  7.6 9.7 %all-to-all-start = ((f32[4,9,8,128]{3,2,1,0:T(8,128)}), f32[4,9,8,128]{3,2,1,0:T(8,128)S(1)}, u32[]{:S(2)}, u32[]{:S(2)}) async-start(f32[4,9,8,128]{3,2,1,0:T(8,128)} %left_phase.1), calls=%async_computation | async-start | bytes 294912 | tf_op jit(solution)/shard_map/all_to_all | solution.py:197
  17.3 0.7 copy-start.1
  22.2 16.1 %collective-permute-start = (f32[97,8,128]{2,1,0:T(8,128)}, f32[97,8,128]{2,1,0:T(8,128)S(1)}, u32[]{:S(2)}, u32[]{:S(2)}) collective-permute-start(f32[97,8,128]{2,1,0:T(8,128)} %get-tuple-element.5), channel_id=1, source_target_pairs={{0,4},{4,0},{1,5},{5,1},{2,6},{6,2},{3,7},{7,3},{8,12},{12,8},{9,1... | collective-permute-start | bytes 1191944 | tf_op jit(solution)/shard_map/ppermute | solution.py:201
  39.4 74.9 %copy-start = (f32[32,6144]{1,0:T(8,128)S(1)}, f32[32,6144]{1,0:T(8,128)}, u32[]{:S(2)}) copy-start(f32[32,6144]{1,0:T(8,128)} %right_ref.5) | copy-start | bytes 2359300
  58.6 21.1 %all-to-all-start.2 = ((f32[12,2,8,128]{3,2,1,0:T(8,128)}), f32[12,2,8,128]{3,2,1,0:T(8,128)S(1)}, u32[]{:S(2)}, u32[]{:S(2)}) async-start(f32[12,2,8,128]{3,2,1,0:T(8,128)} %pad_maximum_fusion.1), calls=%async_computation.2 | async-start | bytes 196608 | tf_op jit(solution)/shard_map/all_to_all | solution.py:211
  106.9 7.4 %collective-permute-start.1 = (f32[4,24,8,128]{3,2,1,0:T(8,128)S(1)}, f32[4,24,8,128]{3,2,1,0:T(8,128)S(1)}, u32[]{:S(2)}, u32[]{:S(2)}) collective-permute-start(f32[4,24,8,128]{3,2,1,0:T(8,128)S(1)} %bitcast.21), channel_id=1, source_target_pairs={{0,4},{4,0},{1,5},{5,1},{2,6},{6,2},{3,7},{7,3},{8,12},{12,8},{9,1... | collective-permute-start | bytes 1179656 | tf_op jit(solution)/shard_map/ppermute | solution.py:218

commit v3 on v0

v3 whole, which is shorter than its diff:
```python
import functools

import jax
import jax.numpy as jnp
from jax import lax
from jax.experimental import pallas as pl
from jax.experimental.pallas import tpu as pltpu
from jax.sharding import Mesh, PartitionSpec as P

SUB, LANE = 8, 128
F32, BF16 = jnp.float32, jnp.bfloat16
NT = (((1,), (1,)), ((), ()))


def split(x):
    high = x.astype(BF16)
    return high, (x - high.astype(F32)).astype(BF16)


def dot(a, b):
    return jnp.dot(a, b, preferred_element_type=F32)


def stack_left(left):
    rank = left.shape[0]
    wide = jnp.concatenate([left] * 4, axis=0).T
    high = wide.astype(BF16).astype(F32)
    lane = lax.broadcasted_iota(jnp.int32, wide.shape, 1)
    return jnp.where(lane < 2 * rank, high, wide - high).astype(BF16)


def pack_column(column):
    bands = column.shape[0] // SUB
    lane = lax.broadcasted_iota(jnp.int32, (SUB, LANE), 1) // (LANE // bands)
    tile = jnp.zeros((SUB, LANE), F32)
    for b in range(bands):
        tile = jnp.where(lane == b, column[b * SUB : (b + 1) * SUB], tile)
    return tile


def unpack_column(tile, bands):
    lane = lax.broadcasted_iota(jnp.int32, (SUB, LANE), 1) // (LANE // bands)
    return [jnp.max(jnp.where(lane == b, tile, 0.0), axis=1, keepdims=True) for b in range(bands)]


def quotient_of(stacked, right, cells):
    high, low = split(right)
    product = dot(stacked, jnp.concatenate([high, low, high, low], axis=0))
    return high, low, split(cells.astype(F32) / product)


def left_kernel(matrix_ref, left_ref, right_ref, out_ref):
    rank, rows = left_ref.shape
    cols = right_ref.shape[1]
    width, chunk = widths(cols)
    stacked = stack_left(left_ref[...])

    def body(i, carry):
        added, summed = carry
        for c in range(width // chunk):
            at = pl.ds(pl.multiple_of(i * width + c * chunk, chunk), chunk)
            right = right_ref[:, at]
            high, low, (q_high, q_low) = quotient_of(stacked, right, matrix_ref[:, at])
            both = lax.dot_general(
                jnp.concatenate([high, low], axis=0), q_high, NT, preferred_element_type=F32
            )
            rest = lax.dot_general(high, q_low, NT, preferred_element_type=F32)
            added += both[:rank] + both[rank:] + rest
            summed += sum(right[:, s : s + LANE] for s in range(0, chunk, LANE))
        return added, summed

    total, mass = lax.fori_loop(
        0, cols // width, body, (jnp.zeros((rank, rows), F32), jnp.zeros((rank, LANE), F32))
    )
    bands, strips = rank // SUB, rows // LANE
    packed = pack_column(jnp.sum(mass, axis=1, keepdims=True))
    for peer in range(out_ref.shape[0]):
        for b in range(bands):
            for s in range(strips):
                out_ref[peer, b * strips + s] = total[b * SUB : (b + 1) * SUB, s * LANE : (s + 1) * LANE]
        out_ref[peer, bands * strips] = packed


def right_kernel(first, half_ref, matrix_ref, left_ref, right_ref, *refs):
    rank, rows = left_ref.shape
    bands, strips = rank // SUB, rows // LANE
    if first:
        source_ref, out_ref, kept_ref, new_ref = refs
        got = sum(source_ref[peer] for peer in range(source_ref.shape[0]))
        masses = unpack_column(got[bands * strips], bands)
        for b in range(bands):
            for s in range(strips):
                at = (slice(b * SUB, (b + 1) * SUB), slice(s * LANE, (s + 1) * LANE))
                value = left_ref[at] * got[b * strips + s] / masses[b]
                new_ref[at] = value
                kept_ref[at] = value
        new = kept_ref[...]
    else:
        (out_ref,) = refs
        new = left_ref[...]
    stacked = stack_left(new)
    new_high, new_low = split(new)
    pair = jnp.concatenate([new_high, new_low], axis=0)

    half = right_ref.shape[1] // 2
    width, chunk = widths(half)
    per_band = half // LANE
    wide = chunk // LANE
    sums = jnp.sum(new, axis=1, keepdims=True)
    for b in range(bands):
        out_ref[bands * per_band + b] = jnp.broadcast_to(sums[b * SUB : (b + 1) * SUB], (SUB, LANE))
    start = half_ref[0] * half

    def body(i, carry):
        for c in range(width // chunk):
            at = pl.ds(pl.multiple_of(start + i * width + c * chunk, chunk), chunk)
            _, _, (q_high, q_low) = quotient_of(stacked, right_ref[:, at], matrix_ref[:, at])
            both = dot(pair, q_high)
            total = both[:rank] + both[rank:] + dot(new_high, q_low)
            for b in range(bands):
                for s in range(wide):
                    out_ref[b * per_band + i * (width // LANE) + c * wide + s] = total[
                        b * SUB : (b + 1) * SUB, s * LANE : (s + 1) * LANE
                    ]
        return carry

    lax.fori_loop(0, half // width, body, 0)


def widths(cols):
    width = 1024 if cols % 1024 == 0 else LANE
    return width, min(width, 256)


def cost(rows, cols, rank):
    return pl.CostEstimate(
        flops=14 * rows * cols * rank, bytes_accessed=2 * rows * cols + 8 * rank * cols, transcendentals=rows * cols
    )


ON_CHIP = pl.BlockSpec(memory_space=pltpu.VMEM)
PARAMS = pltpu.CompilerParams(vmem_limit_bytes=32 << 20)


def left_phase(matrix, left_t, right, n_col):
    (rank, rows), cols = left_t.shape, right.shape[1]
    n_tiles = rank * rows // (SUB * LANE) + 1
    return pl.pallas_call(
        left_kernel,
        name="left_phase",
        out_shape=jax.ShapeDtypeStruct((n_col, n_tiles, SUB, LANE), F32),
        in_specs=[ON_CHIP] * 3,
        out_specs=ON_CHIP,
        compiler_params=PARAMS,
        cost_estimate=cost(rows, cols, rank),
    )(matrix, left_t, right)


def right_phase(half, matrix, left_t, right, *source):
    (rank, rows), cols = left_t.shape, right.shape[1] // 2
    n_tiles = rank * cols // (SUB * LANE) + rank // SUB
    out_shape = [jax.ShapeDtypeStruct((n_tiles, SUB, LANE), F32)]
    if source:
        out_shape += [jax.ShapeDtypeStruct((rank, rows), F32)] * 2
    return pl.pallas_call(
        functools.partial(right_kernel, bool(source)),
        name="right_first" if source else "right_second",
        out_shape=out_shape,
        in_specs=[pl.BlockSpec(memory_space=pltpu.SMEM)] + [ON_CHIP] * (3 + len(source)),
        out_specs=[ON_CHIP] * len(out_shape),
        compiler_params=PARAMS,
        cost_estimate=cost(rows, cols, rank),
    )(half, matrix, left_t, right, *source)


def local(matrix, left_t, right):
    rank, cols = right.shape
    n_col, n_group = lax.axis_size("x"), lax.axis_size(("y", "zl"))
    n_far = lax.axis_size("zh")
    core = lax.axis_index("c")
    partner = [(0, 1), (1, 0)]
    own = jnp.reshape(core, (1,)).astype(jnp.int32)
    other = 1 - own
    left_t, own, other = lax.optimization_barrier((left_t, own, other))

    got = lax.all_to_all(left_phase(matrix, left_t, right, n_col), "x", 0, 0)
    for_partner, kept, new_left_t = right_phase(other, matrix, left_t, right, got)
    there = lax.ppermute(for_partner, "c", partner)
    (here,) = right_phase(own, matrix, kept, right)

    bands, strips = rank // SUB, cols // (2 * LANE)
    half = bands * strips
    each = half // n_group
    summed = here + there
    masses = jnp.repeat(summed[half:], n_group // bands, axis=0)[:, None]
    message = jnp.concatenate([summed[:half].reshape(n_group, each, SUB, LANE), masses], axis=1)
    part = jnp.sum(lax.all_to_all(message, ("y", "zl"), 0, 0), axis=0)
    part = jnp.broadcast_to(part[None], (n_far, each + 1, SUB, LANE))
    part = jnp.sum(lax.all_to_all(part, "zh", 0, 0), axis=0)
    done = part[:each] / part[each:]
    done = jnp.broadcast_to(done[None], (n_group, each, SUB, LANE))
    mine = lax.all_to_all(done, ("y", "zl"), 0, 0).reshape(bands, strips, SUB, LANE)
    theirs = lax.ppermute(mine, "c", partner)
    is_first = own[0] == 0
    low = jnp.where(is_first, mine, theirs)
    high = jnp.where(is_first, theirs, mine)
    whole = jnp.concatenate([low, high], axis=1).transpose(0, 2, 1, 3).reshape(rank, cols)
    return new_left_t, right * whole


def factor(mesh):
    n_row, n_col = mesh.shape["row"], mesh.shape["col"]
    n_far, n_near = (3, 4) if n_row % 24 == 0 else (1, 2)
    shape = (n_row // (2 * n_far * n_near), n_far, n_near, 2, n_col)
    return Mesh(mesh.devices.reshape(shape), ("y", "zh", "zl", "c", "x"))


def solution(mesh):
    row = ("y", "zh", "zl", "c")
    return jax.shard_map(
        local,
        mesh=factor(mesh),
        in_specs=(P(row, "x"), P(None, row), P(None, "x")),
        out_specs=(P(None, row), P(None, "x")),
        check_vma=False,
    )
```

time: 441 us -> 100 us (0.23)
  blocking collectives: 398 us -> 66.2 us
  matrix products: 24.9 us -> 0 us
  starting transfers between devices: 0.04 us -> 16.8 us
  between operations: 14.1 us -> 0.74 us
  Pallas kernels: 0 us -> 9.71 us
    psum x2 -> x0, blocking collectives: 398 us -> none  [the longest x1 384 us: local(): totals, left_mass = lax.psum((partial_sums, local_mass), 'row')]
    all_to_all x0 -> x4, blocking collectives: none -> 66.2 us  [the longest x1 20.9 us: local(): part = jnp.sum(lax.all_to_all(message, ('y', 'zl'), 0, 0), axis=0)]
    dot_general x4 -> x0, matrix products: 24.9 us -> none  [the longest x1 7.62 us: local(): lax.dot_general(left_t, right, (((0,), (0,)), ((), ())), precision=HIGH,...]
    ppermute x0 -> x2, starting transfers between devices: none -> 16.8 us  [the longest x1 11.2 us: local(): there = lax.ppermute(for_partner, 'c', partner)]
    pallas_call x0 -> x3, Pallas kernels: none -> 9.71 us  [the longest x1 5.65 us: left_phase(): pl.pallas_call(left_kernel, name='left_phase', out_shape=jax.ShapeDtypeSt...]
  transfers between devices with their start and end apart: 1 -> 2, of which waited for: 0 -> 1; matrix products, arithmetic and copies ran while one was open for 0% -> 0% of each run, Pallas kernels for 0% -> 2%
where the time goes in v3:
time: 100 us; the launch traced here: 99.8 us
  blocking collectives  66.2 us (66%)
  starting transfers between devices  16.8 us (17%)
  Pallas kernels  9.71 us (10%)
  local copies, waits for them, and re-layouts  3.86 us (4%)
  waiting for transfers between devices  1.33 us (1%)
  other arithmetic  1.18 us (1%)
    all_to_all x1, blocking collectives, local(): part = jnp.sum(lax.all_to_all(message, ('y', 'zl'), 0, 0), axis=0)  20.9 us
    all_to_all x1, blocking collectives, local(): lax.all_to_all(done, ('y', 'zl'), 0, 0).reshape(bands, strips, SUB, LANE)  18.3 us
    all_to_all x1, blocking collectives, local(): part = jnp.sum(lax.all_to_all(part, 'zh', 0, 0), axis=0)  17.4 us
    ppermute x1, starting transfers between devices, local(): there = lax.ppermute(for_partner, 'c', partner)  11.2 us
    all_to_all x1, blocking collectives, local(): got = lax.all_to_all(left_phase(matrix, left_t, right, n_col), 'x', 0, 0)  9.67 us
    pallas_call x1, Pallas kernels, left_phase(): pl.pallas_call(left_kernel, name='left_phase', out_shape=jax.ShapeDtypeSt...  5.65 us
    ppermute x1, starting transfers between devices, local(): theirs = lax.ppermute(mine, 'c', partner)  5.52 us
    pallas_call x2, Pallas kernels, right_phase(): pl.pallas_call(functools.partial(right_kernel, bool(source)), name='right...  4.06 us
  transfers between devices with their start and end apart: 2, of which 1 were waited for; matrix products, arithmetic and copies ran while one was open for 0% of the time, Pallas kernels for 2%

profile of v3, /device:TPU:1, one launch (start us, length us, event | category | flops | bytes accessed | tf_op | source)
XLA Modules:
  0.0 99.8 jit_solution(2995960638942677573)
XLA Ops:
  0.6 0.0 copy-start
  0.6 1.9 %copy-done = bf16[256,6144]{1,0:T(8,128)(2,1)S(1)} copy-done((bf16[256,6144]{1,0:T(8,128)(2,1)S(1)}, bf16[256,6144]{1,0:T(8,128)(2,1)}, u32[]{:S(2)}) %copy-start) | copy-done | bytes 3145752
  2.5 0.0 copy-start.1
  2.5 1.1 %copy-done.1 = f32[32,6144]{1,0:T(8,128)S(1)} copy-done((f32[32,6144]{1,0:T(8,128)S(1)}, f32[32,6144]{1,0:T(8,128)}, u32[]{:S(2)}) %copy-start.1) | copy-done | bytes 786456
  3.7 0.0 copy-start.3
  3.7 0.8 copy-done.3
  4.4 5.6 %left_phase.1 = f32[4,9,8,128]{3,2,1,0:T(8,128)S(1)} custom-call(bf16[256,6144]{1,0:T(8,128)(2,1)S(1)} %copy-done, f32[32,256]{1,0:T(8,128)S(1)} %copy-done.3, f32[32,6144]{1,0:T(8,128)S(1)} %copy-done.1), custom_call_target="tpu_custom_call" | custom-call | flops 704643072 | bytes 4718592 | tf_op jit(solution)/shard_map/left_phase/pallas_call | solution.py:148
  10.1 0.0 copy-start.2
  10.1 9.7 %all_to_all.20.refs_0_ = f32[4,9,8,128]{3,2,1,0:T(8,128)S(1)} all-to-all(f32[4,9,8,128]{3,2,1,0:T(8,128)S(1)} %left_phase.1), channel_id=1, replica_groups=mesh['y'=8,'zh'=3,'zl'=4,'c'=2,'x'=4] {'x'}, dimensions={0} | all-to-all | bytes 294912 | tf_op jit(solution)/shard_map/all_to_all | solution.py:186
  19.7 2.2 %right_first.1 = (f32[100,8,128]{2,1,0:T(8,128)S(1)}, f32[32,256]{1,0:T(8,128)S(1)}, f32[32,256]{1,0:T(8,128)}) custom-call(s32[1]{0:T(128)S(6)} %sub.3.half_ref, bf16[256,6144]{1,0:T(8,128)(2,1)S(1)} %copy-done, f32[32,256]{1,0:T(8,128)S(1)} %copy-done.3, f32[32,6144]{1,0:T(8,128)S(1)} %copy-done.1, f32[4,9,8,128]{3,2,1,0:T(8,128)S(1)} %all_to_all.20.refs_0_), custom_call_target="tpu_custom_call" | custom-call | flops 352321536 | bytes 2359296 | tf_op jit(solution)/shard_map/right_first/pallas_call | solution.py:165
  21.9 11.2 %collective-permute-start = (f32[100,8,128]{2,1,0:T(8,128)S(1)}, f32[100,8,128]{2,1,0:T(8,128)S(1)}, u32[]{:S(2)}, u32[]{:S(2)}) collective-permute-start(f32[100,8,128]{2,1,0:T(8,128)S(1)} %get-tuple-element.13), channel_id=1, source_target_pairs={{0,4},{4,0},{1,5},{5,1},{2,6},{6,2},{3,7},{7,3},{8,12},{12,8},{9,1... | collective-permute-start | bytes 1228808 | tf_op jit(solution)/shard_map/ppermute | solution.py:188
  33.2 0.0 copy-done.2
  33.2 1.9 %right_second.1 = f32[100,8,128]{2,1,0:T(8,128)S(1)} custom-call(s32[1]{0:T(128)} %bitcast.half_ref, bf16[256,6144]{1,0:T(8,128)(2,1)S(1)} %copy-done, f32[32,256]{1,0:T(8,128)S(1)} %get-tuple-element.12.left_ref, f32[32,6144]{1,0:T(8,128)S(1)} %copy-done.2), custom_call_target="tpu_custom_call" | custom-call | flops 352321536 | bytes 2359296 | tf_op jit(solution)/shard_map/right_second/pallas_call | solution.py:165
  35.1 0.0 collective-permute-done
  35.1 0.1 add.3
  35.2 20.9 %all_to_all.21 = f32[32,4,8,128]{3,2,1,0:T(8,128)S(1)} all-to-all(f32[32,4,8,128]{3,2,1,0:T(8,128)S(1)} %pad_maximum_fusion), channel_id=1, replica_groups=mesh['y'=8,'zh'=3,'zl'=4,'c'=2,'x'=4] {'y','zl'}, dimensions={0} | all-to-all | bytes 1048576 | tf_op jit(solution)/shard_map/all_to_all | solution.py:197
  56.2 17.4 %all_to_all.22 = f32[3,4,8,128]{3,2,1,0:T(8,128)S(1)} all-to-all(f32[3,4,8,128]{3,2,1,0:T(8,128)S(1)} %broadcast_in_dim.7), channel_id=1, replica_groups=mesh['y'=8,'zh'=3,'zl'=4,'c'=2,'x'=4] {'zh'}, dimensions={0} | all-to-all | bytes 98304 | tf_op jit(solution)/shard_map/all_to_all | solution.py:199
  73.7 18.3 %all_to_all.23 = f32[32,3,8,128]{3,2,1,0:T(8,128)S(1)} all-to-all(f32[32,3,8,128]{3,2,1,0:T(8,128)S(1)} %broadcast_in_dim.8), channel_id=1, replica_groups=mesh['y'=8,'zh'=3,'zl'=4,'c'=2,'x'=4] {'y','zl'}, dimensions={0} | all-to-all | bytes 786432 | tf_op jit(solution)/shard_map/all_to_all | solution.py:202
  91.9 5.5 %collective-permute-start.1 = (f32[4,24,8,128]{3,2,1,0:T(8,128)S(1)}, f32[4,24,8,128]{3,2,1,0:T(8,128)S(1)}, u32[]{:S(2)}, u32[]{:S(2)}) collective-permute-start(f32[4,24,8,128]{3,2,1,0:T(8,128)S(1)} %bitcast.16), channel_id=1, source_target_pairs={{0,4},{4,0},{1,5},{5,1},{2,6},{6,2},{3,7},{7,3},{8,12},{12,8},{9,1... | collective-permute-start | bytes 1179656 | tf_op jit(solution)/shard_map/ppermute | solution.py:203
  97.5 1.3 %collective-permute-done.1 = f32[4,24,8,128]{3,2,1,0:T(8,128)S(1)} collective-permute-done((f32[4,24,8,128]{3,2,1,0:T(8,128)S(1)}, f32[4,24,8,128]{3,2,1,0:T(8,128)S(1)}, u32[]{:S(2)}, u32[]{:S(2)}) %collective-permute-start.1) | collective-permute-done | bytes 393248 | tf_op jit(solution)/shard_map/ppermute | solution.py:203
  98.8 0.1 broadcast_select_fusion.1
  98.9 1.0 fusion
  (10 shorter events, 0.2 us)
Async XLA Ops:
  0.6 1.9 %copy-start = (bf16[256,6144]{1,0:T(8,128)(2,1)S(1)}, bf16[256,6144]{1,0:T(8,128)(2,1)}, u32[]{:S(2)}) copy-start(bf16[256,6144]{1,0:T(8,128)(2,1)} %matrix_ref.5) | copy-start | bytes 9437188
  2.5 1.1 %copy-start.1 = (f32[32,6144]{1,0:T(8,128)S(1)}, f32[32,6144]{1,0:T(8,128)}, u32[]{:S(2)}) copy-start(f32[32,6144]{1,0:T(8,128)} %right_ref.5) | copy-start | bytes 2359300
  3.7 0.8 copy-start.3
  10.1 23.1 %copy-start.2 = (f32[32,6144]{1,0:T(8,128)S(1)}, f32[32,6144]{1,0:T(8,128)}, u32[]{:S(2)}) copy-start(f32[32,6144]{1,0:T(8,128)} %right_ref.5) | copy-start | bytes 2359300
  21.9 13.1 %collective-permute-start = (f32[100,8,128]{2,1,0:T(8,128)S(1)}, f32[100,8,128]{2,1,0:T(8,128)S(1)}, u32[]{:S(2)}, u32[]{:S(2)}) collective-permute-start(f32[100,8,128]{2,1,0:T(8,128)S(1)} %get-tuple-element.13), channel_id=1, source_target_pairs={{0,4},{4,0},{1,5},{5,1},{2,6},{6,2},{3,7},{7,3},{8,12},{12,8},{9,1... | collective-permute-start | bytes 1228808 | tf_op jit(solution)/shard_map/ppermute | solution.py:188
  91.9 6.9 %collective-permute-start.1 = (f32[4,24,8,128]{3,2,1,0:T(8,128)S(1)}, f32[4,24,8,128]{3,2,1,0:T(8,128)S(1)}, u32[]{:S(2)}, u32[]{:S(2)}) collective-permute-start(f32[4,24,8,128]{3,2,1,0:T(8,128)S(1)} %bitcast.16), channel_id=1, source_target_pairs={{0,4},{4,0},{1,5},{5,1},{2,6},{6,2},{3,7},{7,3},{8,12},{12,8},{9,1... | collective-permute-start | bytes 1179656 | tf_op jit(solution)/shard_map/ppermute | solution.py:203

commit v4 on v3

--- a/solution.py
+++ b/solution.py
@@ -8,6 +8,7 @@
 from jax.sharding import Mesh, PartitionSpec as P
 
 SUB, LANE = 8, 128
+ROWS_OF = 2
 F32, BF16 = jnp.float32, jnp.bfloat16
 NT = (((1,), (1,)), ((), ()))
 
@@ -49,29 +50,47 @@
     return high, low, split(cells.astype(F32) / product)
 
 
-def left_kernel(matrix_ref, left_ref, right_ref, out_ref):
+def left_kernel(matrix_hbm, left_ref, right_ref, out_ref, matrix_ref, both_ref, rest_ref, sems):
     rank, rows = left_ref.shape
     cols = right_ref.shape[1]
     width, chunk = widths(cols)
+    steps = cols // width
+
+    def fetch(i):
+        at = pl.ds(pl.multiple_of(i * width, width), width)
+        return pltpu.make_async_copy(matrix_hbm.at[:, at], matrix_ref.at[:, at], sems.at[i])
+
+    for i in range(steps):
+        fetch(i).start()
+    both_ref[...] = jnp.zeros_like(both_ref)
+    rest_ref[...] = jnp.zeros_like(rest_ref)
     stacked = stack_left(left_ref[...])
 
-    def body(i, carry):
-        added, summed = carry
+    def body(i, summed):
+        fetch(i).wait()
+        highs, lows, q_highs, q_lows = [], [], [], []
         for c in range(width // chunk):
             at = pl.ds(pl.multiple_of(i * width + c * chunk, chunk), chunk)
             right = right_ref[:, at]
             high, low, (q_high, q_low) = quotient_of(stacked, right, matrix_ref[:, at])
-            both = lax.dot_general(
-                jnp.concatenate([high, low], axis=0), q_high, NT, preferred_element_type=F32
-            )
-            rest = lax.dot_general(high, q_low, NT, preferred_element_type=F32)
-            added += both[:rank] + both[rank:] + rest
+            highs.append(high)
+            lows.append(low)
+            q_highs.append(q_high)
+            q_lows.append(q_low)
             summed += sum(right[:, s : s + LANE] for s in range(0, chunk, LANE))
-        return added, summed
-
-    total, mass = lax.fori_loop(
-        0, cols // width, body, (jnp.zeros((rank, rows), F32), jnp.zeros((rank, LANE), F32))
-    )
+        high = jnp.concatenate(highs, axis=1)
+        low = jnp.concatenate(lows, axis=1)
+        both_ref[...] += lax.dot_general(
+            jnp.concatenate(q_highs, axis=1), jnp.concatenate([high, low], axis=0), NT, preferred_element_type=F32
+        )
+        rest_ref[...] += lax.dot_general(
+            jnp.concatenate(q_lows, axis=1), high, NT, preferred_element_type=F32
+        )
+        return summed
+
+    mass = lax.fori_loop(0, steps, body, jnp.zeros((rank, LANE), F32))
+    both = both_ref[...].T
+    total = both[:rank] + both[rank:] + rest_ref[...].T
     bands, strips = rank // SUB, rows // LANE
     packed = pack_column(jnp.sum(mass, axis=1, keepdims=True))
     for peer in range(out_ref.shape[0]):
@@ -127,6 +146,51 @@
     lax.fori_loop(0, half // width, body, 0)
 
 
+def message_kernel(here_ref, there_ref, out_ref):
+    peers, pairs = out_ref.shape[0], out_ref.shape[1] - 1
+    per_tile = SUB // ROWS_OF
+    each = pairs // per_tile
+    half = peers * each
+    bands = here_ref.shape[0] - half
+    group = lax.broadcasted_iota(jnp.int32, (ROWS_OF, LANE), 1) // (LANE // per_tile)
+    for b in range(bands):
+        mass = here_ref[half + b] + there_ref[half + b]
+        packed = jnp.zeros((ROWS_OF, LANE), F32)
+        for r in range(per_tile):
+            packed = jnp.where(group == r, mass[r * ROWS_OF : (r + 1) * ROWS_OF], packed)
+        for p in range(b * peers // bands, (b + 1) * peers // bands):
+            out_ref[p, pairs] = packed
+    for t in range(half):
+        tile = here_ref[t] + there_ref[t]
+        for r in range(per_tile):
+            out_ref[t // each, t % each * per_tile + r] = tile[r * ROWS_OF : (r + 1) * ROWS_OF]
+
+
+def finish_kernel(part_ref, out_ref):
+    per_tile = SUB // ROWS_OF
+    pairs = part_ref.shape[1] - 1
+    group = lax.broadcasted_iota(jnp.int32, (ROWS_OF, LANE), 1) // (LANE // per_tile)
+    rows = [sum(part_ref[f, i] for f in range(part_ref.shape[0])) for i in range(pairs + 1)]
+    mass = jnp.concatenate(
+        [jnp.max(jnp.where(group == r, rows[pairs], 0.0), axis=1, keepdims=True) for r in range(per_tile)], axis=0
+    )
+    for e in range(out_ref.shape[1]):
+        tile = jnp.concatenate(rows[e * per_tile : (e + 1) * per_tile], axis=0) / mass
+        for p in range(out_ref.shape[0]):
+            out_ref[p, e] = tile
+
+
+def on_chip(kernel, name, shape, *args):
+    return pl.pallas_call(
+        kernel,
+        name=name,
+        out_shape=jax.ShapeDtypeStruct(shape, F32),
+        in_specs=[ON_CHIP] * len(args),
+        out_specs=ON_CHIP,
+        compiler_params=PARAMS,
+    )(*args)
+
+
 def widths(cols):
     width = 1024 if cols % 1024 == 0 else LANE
     return width, min(width, 256)
@@ -138,20 +202,30 @@
     )
 
 
+LEFT_LIMIT = 51_000_000
 ON_CHIP = pl.BlockSpec(memory_space=pltpu.VMEM)
 PARAMS = pltpu.CompilerParams(vmem_limit_bytes=32 << 20)
 
 
 def left_phase(matrix, left_t, right, n_col):
     (rank, rows), cols = left_t.shape, right.shape[1]
+    steps = cols // widths(cols)[0]
     n_tiles = rank * rows // (SUB * LANE) + 1
     return pl.pallas_call(
         left_kernel,
         name="left_phase",
-        out_shape=jax.ShapeDtypeStruct((n_col, n_tiles, SUB, LANE), F32),
-        in_specs=[ON_CHIP] * 3,
-        out_specs=ON_CHIP,
-        compiler_params=PARAMS,
+        out_shape=[
+            jax.ShapeDtypeStruct((n_col, n_tiles, SUB, LANE), F32),
+            jax.ShapeDtypeStruct(matrix.shape, matrix.dtype),
+        ],
+        in_specs=[pl.BlockSpec(memory_space=pltpu.HBM), ON_CHIP, ON_CHIP],
+        out_specs=[ON_CHIP] * 2,
+        scratch_shapes=[
+            pltpu.VMEM((rows, 2 * rank), F32),
+            pltpu.VMEM((rows, rank), F32),
+            pltpu.SemaphoreType.DMA((steps,)),
+        ],
+        compiler_params=pltpu.CompilerParams(vmem_limit_bytes=LEFT_LIMIT),
         cost_estimate=cost(rows, cols, rank),
     )(matrix, left_t, right)
 
@@ -183,7 +257,8 @@
     other = 1 - own
     left_t, own, other = lax.optimization_barrier((left_t, own, other))
 
-    got = lax.all_to_all(left_phase(matrix, left_t, right, n_col), "x", 0, 0)
+    sent, matrix = left_phase(matrix, left_t, right, n_col)
+    got = lax.all_to_all(sent, "x", 0, 0)
     for_partner, kept, new_left_t = right_phase(other, matrix, left_t, right, got)
     there = lax.ppermute(for_partner, "c", partner)
     (here,) = right_phase(own, matrix, kept, right)
@@ -191,14 +266,11 @@
     bands, strips = rank // SUB, cols // (2 * LANE)
     half = bands * strips
     each = half // n_group
-    summed = here + there
-    masses = jnp.repeat(summed[half:], n_group // bands, axis=0)[:, None]
-    message = jnp.concatenate([summed[:half].reshape(n_group, each, SUB, LANE), masses], axis=1)
+    pairs = each * (SUB // ROWS_OF)
+    message = on_chip(message_kernel, "message", (n_group, pairs + 1, ROWS_OF, LANE), here, there)
     part = jnp.sum(lax.all_to_all(message, ("y", "zl"), 0, 0), axis=0)
-    part = jnp.broadcast_to(part[None], (n_far, each + 1, SUB, LANE))
-    part = jnp.sum(lax.all_to_all(part, "zh", 0, 0), axis=0)
-    done = part[:each] / part[each:]
-    done = jnp.broadcast_to(done[None], (n_group, each, SUB, LANE))
+    part = lax.all_to_all(jnp.broadcast_to(part[None], (n_far, *part.shape)), "zh", 0, 0)
+    done = on_chip(finish_kernel, "finish", (n_group, each, SUB, LANE), part)
     mine = lax.all_to_all(done, ("y", "zl"), 0, 0).reshape(bands, strips, SUB, LANE)
     theirs = lax.ppermute(mine, "c", partner)
     is_first = own[0] == 0

time: 100 us -> 95.4 us (0.954)
  blocking collectives: 66.2 us -> 64.2 us
  local copies, waits for them, and re-layouts: 3.86 us -> 1.9 us
    unnamed x8 -> x6, local copies, waits for them, and re-layouts: 3.78 us -> 1.89 us
    all_to_all x1, blocking collectives: 20.9 us -> 19.6 us  [local(): part = jnp.sum(lax.all_to_all(message, ('y', 'zl'), 0, 0), axis=0)]
    pallas_call x1 -> x3, Pallas kernels: 5.65 us -> 4.94 us  [the longest x1 4.7 us: left_phase(): pl.pallas_call(left_kernel, name='left_phase', out_shape=[jax.ShapeDtypeS...]
where the time goes in v4:
time: 95.4 us; the launch traced here: 95 us
  blocking collectives  64.2 us (67%)
  starting transfers between devices  16.7 us (18%)
  Pallas kernels  9 us (9%)
  local copies, waits for them, and re-layouts  1.9 us (2%)
  waiting for transfers between devices  1.34 us (1%)
  other arithmetic  1.15 us (1%)
    all_to_all x1, blocking collectives, local(): part = jnp.sum(lax.all_to_all(message, ('y', 'zl'), 0, 0), axis=0)  19.6 us
    all_to_all x1, blocking collectives, local(): lax.all_to_all(done, ('y', 'zl'), 0, 0).reshape(bands, strips, SUB, LANE)  17.6 us
    all_to_all x1, blocking collectives, local(): lax.all_to_all(jnp.broadcast_to(part[None], (n_far, *part.shape)), 'zh',...  17.4 us
    ppermute x1, starting transfers between devices, local(): there = lax.ppermute(for_partner, 'c', partner)  11.2 us
    all_to_all x1, blocking collectives, local(): got = lax.all_to_all(sent, 'x', 0, 0)  9.55 us
    ppermute x1, starting transfers between devices, local(): theirs = lax.ppermute(mine, 'c', partner)  5.41 us
    pallas_call x1, Pallas kernels, left_phase(): pl.pallas_call(left_kernel, name='left_phase', out_shape=[jax.ShapeDtypeS...  4.7 us
    pallas_call x2, Pallas kernels, right_phase(): pl.pallas_call(functools.partial(right_kernel, bool(source)), name='right...  4.06 us
  transfers between devices with their start and end apart: 2, of which 1 were waited for; matrix products, arithmetic and copies ran while one was open for 0% of the time, Pallas kernels for 2%

profile of v4, /device:TPU:1, one launch (start us, length us, event | category | flops | bytes accessed | tf_op | source)
XLA Modules:
  0.0 95.0 jit_solution(6219932402837334215)
XLA Ops:
  0.6 0.0 copy-start
  0.6 1.1 %copy-done = f32[32,6144]{1,0:T(8,128)S(1)} copy-done((f32[32,6144]{1,0:T(8,128)S(1)}, f32[32,6144]{1,0:T(8,128)}, u32[]{:S(2)}) %copy-start) | copy-done | bytes 786456
  1.8 0.0 copy-start.2
  1.8 0.8 copy-done.2
  2.5 4.7 %left_phase.1 = (f32[4,9,8,128]{3,2,1,0:T(8,128)S(1)}, bf16[256,6144]{1,0:T(8,128)(2,1)S(1)}) custom-call(bf16[256,6144]{1,0:T(8,128)(2,1)} %matrix_hbm.1, f32[32,256]{1,0:T(8,128)S(1)} %copy-done.2, f32[32,6144]{1,0:T(8,128)S(1)} %copy-done), custom_call_target="tpu_custom_call" | custom-call | flops 704643072 | bytes 4718592 | tf_op jit(solution)/shard_map/left_phase/pallas_call | solution.py:214
  7.2 9.5 %all_to_all.20.refs_0_ = f32[4,9,8,128]{3,2,1,0:T(8,128)S(1)} all-to-all(f32[4,9,8,128]{3,2,1,0:T(8,128)S(1)} %get-tuple-element.13), channel_id=1, replica_groups=mesh['y'=8,'zh'=3,'zl'=4,'c'=2,'x'=4] {'x'}, dimensions={0} | all-to-all | bytes 294912 | tf_op jit(solution)/shard_map/all_to_all | solution.py:261
  16.8 2.2 %right_first.1 = (f32[100,8,128]{2,1,0:T(8,128)S(1)}, f32[32,256]{1,0:T(8,128)S(1)}, f32[32,256]{1,0:T(8,128)}) custom-call(s32[1]{0:T(128)S(6)} %sub.3.half_ref, bf16[256,6144]{1,0:T(8,128)(2,1)S(1)} %get-tuple-element.12.matrix_ref, f32[32,256]{1,0:T(8,128)S(1)} %copy-done.2, f32[32,6144]{1,0:T(8,128)S(1)} %copy-done, f32[4,9,8,128]{3,2,1,0:T(8,128)S(1)} %all_to_all.20.refs_0_), custom_call_target="tpu_custom_call" | custom-call | flops 352321536 | bytes 2359296 | tf_op jit(solution)/shard_map/right_first/pallas_call | solution.py:239
  19.0 11.2 %collective-permute-start = (f32[100,8,128]{2,1,0:T(8,128)S(1)}, f32[100,8,128]{2,1,0:T(8,128)S(1)}, u32[]{:S(2)}, u32[]{:S(2)}) collective-permute-start(f32[100,8,128]{2,1,0:T(8,128)S(1)} %get-tuple-element.17), channel_id=1, source_target_pairs={{0,4},{4,0},{1,5},{5,1},{2,6},{6,2},{3,7},{7,3},{8,12},{12,8},{9,1... | collective-permute-start | bytes 1228808 | tf_op jit(solution)/shard_map/ppermute | solution.py:263
  30.2 1.9 %right_second.1.here_ref = f32[100,8,128]{2,1,0:T(8,128)S(1)} custom-call(s32[1]{0:T(128)} %bitcast.half_ref, bf16[256,6144]{1,0:T(8,128)(2,1)S(1)} %get-tuple-element.12.matrix_ref, f32[32,256]{1,0:T(8,128)S(1)} %get-tuple-element.16.left_ref, f32[32,6144]{1,0:T(8,128)S(1)} %copy-done), custom_call_target="tpu_custom_call" | custom-call | flops 352321536 | bytes 2359296 | tf_op jit(solution)/shard_map/right_second/pallas_call | solution.py:239
  32.1 0.0 copy-start.1
  32.1 0.0 collective-permute-done.there_ref
  32.2 19.6 %all_to_all.21 = f32[32,13,2,128]{3,2,1,0:T(2,128)S(1)} all-to-all(f32[32,13,2,128]{3,2,1,0:T(2,128)S(1)} %message.1), channel_id=1, replica_groups=mesh['y'=8,'zh'=3,'zl'=4,'c'=2,'x'=4] {'y','zl'}, dimensions={0} | all-to-all | bytes 851968 | tf_op jit(solution)/shard_map/all_to_all | solution.py:271
  51.8 0.1 reduce_sum.9
  52.0 17.4 %all_to_all.22.part_ref = f32[3,13,2,128]{3,2,1,0:T(2,128)S(1)} all-to-all(f32[3,13,2,128]{3,2,1,0:T(2,128)S(1)} %broadcast_in_dim.2), channel_id=1, replica_groups=mesh['y'=8,'zh'=3,'zl'=4,'c'=2,'x'=4] {'zh'}, dimensions={0} | all-to-all | bytes 79872 | tf_op jit(solution)/shard_map/all_to_all | solution.py:272
  69.4 0.2 finish.1
  69.6 17.6 %all_to_all.23 = f32[32,3,8,128]{3,2,1,0:T(8,128)S(1)} all-to-all(f32[32,3,8,128]{3,2,1,0:T(8,128)S(1)} %finish.1), channel_id=1, replica_groups=mesh['y'=8,'zh'=3,'zl'=4,'c'=2,'x'=4] {'y','zl'}, dimensions={0} | all-to-all | bytes 786432 | tf_op jit(solution)/shard_map/all_to_all | solution.py:274
  87.2 5.4 %collective-permute-start.1 = (f32[4,24,8,128]{3,2,1,0:T(8,128)S(1)}, f32[4,24,8,128]{3,2,1,0:T(8,128)S(1)}, u32[]{:S(2)}, u32[]{:S(2)}) collective-permute-start(f32[4,24,8,128]{3,2,1,0:T(8,128)S(1)} %bitcast.12), channel_id=1, source_target_pairs={{0,4},{4,0},{1,5},{5,1},{2,6},{6,2},{3,7},{7,3},{8,12},{12,8},{9,1... | collective-permute-start | bytes 1179656 | tf_op jit(solution)/shard_map/ppermute | solution.py:275
  92.6 1.3 %collective-permute-done.1 = f32[4,24,8,128]{3,2,1,0:T(8,128)S(1)} collective-permute-done((f32[4,24,8,128]{3,2,1,0:T(8,128)S(1)}, f32[4,24,8,128]{3,2,1,0:T(8,128)S(1)}, u32[]{:S(2)}, u32[]{:S(2)}) %collective-permute-start.1) | collective-permute-done | bytes 393248 | tf_op jit(solution)/shard_map/ppermute | solution.py:275
  94.0 0.1 broadcast_select_fusion.1
  94.0 0.0 copy-done.1
  94.0 1.0 %fusion = f32[32,6144]{1,0:T(8,128)} fusion(f32[32,6144]{1,0:T(8,128)S(1)} %copy-done.1, f32[4,24,8,128]{3,2,1,0:T(8,128)S(1)} %get-tuple-element.19, f32[4,24,8,128]{3,2,1,0:T(8,128)S(1)} %get-tuple-element.18), kind=kLoop, calls=%fused_computation.1 | loop fusion | flops 393216 | bytes 2359296 | tf_op jit(solution)/shard_map/mul | solution.py:280
  (2 shorter events, 0.1 us)
Async XLA Ops:
  0.6 1.1 %copy-start = (f32[32,6144]{1,0:T(8,128)S(1)}, f32[32,6144]{1,0:T(8,128)}, u32[]{:S(2)}) copy-start(f32[32,6144]{1,0:T(8,128)} %right_ref.5) | copy-start | bytes 2359300
  1.8 0.8 copy-start.2
  19.0 13.1 %collective-permute-start = (f32[100,8,128]{2,1,0:T(8,128)S(1)}, f32[100,8,128]{2,1,0:T(8,128)S(1)}, u32[]{:S(2)}, u32[]{:S(2)}) collective-permute-start(f32[100,8,128]{2,1,0:T(8,128)S(1)} %get-tuple-element.17), channel_id=1, source_target_pairs={{0,4},{4,0},{1,5},{5,1},{2,6},{6,2},{3,7},{7,3},{8,12},{12,8},{9,1... | collective-permute-start | bytes 1228808 | tf_op jit(solution)/shard_map/ppermute | solution.py:263
  32.1 61.9 %copy-start.1 = (f32[32,6144]{1,0:T(8,128)S(1)}, f32[32,6144]{1,0:T(8,128)}, u32[]{:S(2)}) copy-start(f32[32,6144]{1,0:T(8,128)} %right_ref.5) | copy-start | bytes 2359300
  87.2 6.7 %collective-permute-start.1 = (f32[4,24,8,128]{3,2,1,0:T(8,128)S(1)}, f32[4,24,8,128]{3,2,1,0:T(8,128)S(1)}, u32[]{:S(2)}, u32[]{:S(2)}) collective-permute-start(f32[4,24,8,128]{3,2,1,0:T(8,128)S(1)} %bitcast.12), channel_id=1, source_target_pairs={{0,4},{4,0},{1,5},{5,1},{2,6},{6,2},{3,7},{7,3},{8,12},{12,8},{9,1... | collective-permute-start | bytes 1179656 | tf_op jit(solution)/shard_map/ppermute | solution.py:275

commit v5 on v4

--- a/solution.py
+++ b/solution.py
@@ -50,24 +50,32 @@
     return high, low, split(cells.astype(F32) / product)
 
 
-def left_kernel(matrix_hbm, left_ref, right_ref, out_ref, matrix_ref, both_ref, rest_ref, sems):
+def left_kernel(matrix_hbm, left_hbm, right_hbm, out_ref, matrix_ref, left_ref, right_ref, both_ref, rest_ref, sems, left_sem):
     rank, rows = left_ref.shape
     cols = right_ref.shape[1]
     width, chunk = widths(cols)
     steps = cols // width
 
-    def fetch(i):
+    def fetches(i):
         at = pl.ds(pl.multiple_of(i * width, width), width)
-        return pltpu.make_async_copy(matrix_hbm.at[:, at], matrix_ref.at[:, at], sems.at[i])
-
+        return (
+            pltpu.make_async_copy(right_hbm.at[:, at], right_ref.at[:, at], sems.at[0, i]),
+            pltpu.make_async_copy(matrix_hbm.at[:, at], matrix_ref.at[:, at], sems.at[1, i]),
+        )
+
+    fetch_left = pltpu.make_async_copy(left_hbm, left_ref, left_sem)
+    fetch_left.start()
     for i in range(steps):
-        fetch(i).start()
+        for fetch in fetches(i):
+            fetch.start()
     both_ref[...] = jnp.zeros_like(both_ref)
     rest_ref[...] = jnp.zeros_like(rest_ref)
+    fetch_left.wait()
     stacked = stack_left(left_ref[...])
 
     def body(i, summed):
-        fetch(i).wait()
+        for fetch in fetches(i):
+            fetch.wait()
         highs, lows, q_highs, q_lows = [], [], [], []
         for c in range(width // chunk):
             at = pl.ds(pl.multiple_of(i * width + c * chunk, chunk), chunk)
@@ -166,11 +174,24 @@
             out_ref[t // each, t % each * per_tile + r] = tile[r * ROWS_OF : (r + 1) * ROWS_OF]
 
 
-def finish_kernel(part_ref, out_ref):
+def finish_kernel(place_ref, *refs):
+    *parts, out_ref = refs
+    n = len(parts)
+    far_of = [lax.rem(place_ref[0] - source + n, n) for source in range(n)]
+
+    def ordered(i):
+        total = None
+        for far in far_of:
+            value = parts[0][i]
+            for d in range(1, n):
+                value = jnp.where(far == d, parts[d][i], value)
+            total = value if total is None else total + value
+        return total
+
     per_tile = SUB // ROWS_OF
-    pairs = part_ref.shape[1] - 1
+    pairs = parts[0].shape[0] - 1
     group = lax.broadcasted_iota(jnp.int32, (ROWS_OF, LANE), 1) // (LANE // per_tile)
-    rows = [sum(part_ref[f, i] for f in range(part_ref.shape[0])) for i in range(pairs + 1)]
+    rows = [ordered(i) for i in range(pairs + 1)]
     mass = jnp.concatenate(
         [jnp.max(jnp.where(group == r, rows[pairs], 0.0), axis=1, keepdims=True) for r in range(per_tile)], axis=0
     )
@@ -180,15 +201,16 @@
             out_ref[p, e] = tile
 
 
-def on_chip(kernel, name, shape, *args):
+def on_chip(kernel, name, shape, *args, scalar=None):
+    scalars = () if scalar is None else (scalar,)
     return pl.pallas_call(
         kernel,
         name=name,
         out_shape=jax.ShapeDtypeStruct(shape, F32),
-        in_specs=[ON_CHIP] * len(args),
+        in_specs=[pl.BlockSpec(memory_space=pltpu.SMEM)] * len(scalars) + [ON_CHIP] * len(args),
         out_specs=ON_CHIP,
         compiler_params=PARAMS,
-    )(*args)
+    )(*scalars, *args)
 
 
 def widths(cols):
@@ -202,7 +224,7 @@
     )
 
 
-LEFT_LIMIT = 51_000_000
+LEFT_LIMIT = 32 << 20
 ON_CHIP = pl.BlockSpec(memory_space=pltpu.VMEM)
 PARAMS = pltpu.CompilerParams(vmem_limit_bytes=32 << 20)
 
@@ -217,17 +239,20 @@
         out_shape=[
             jax.ShapeDtypeStruct((n_col, n_tiles, SUB, LANE), F32),
             jax.ShapeDtypeStruct(matrix.shape, matrix.dtype),
+            jax.ShapeDtypeStruct(left_t.shape, F32),
+            jax.ShapeDtypeStruct(right.shape, F32),
         ],
-        in_specs=[pl.BlockSpec(memory_space=pltpu.HBM), ON_CHIP, ON_CHIP],
-        out_specs=[ON_CHIP] * 2,
+        in_specs=[pl.BlockSpec(memory_space=pltpu.HBM)] * 3,
+        out_specs=[ON_CHIP] * 4,
         scratch_shapes=[
             pltpu.VMEM((rows, 2 * rank), F32),
             pltpu.VMEM((rows, rank), F32),
-            pltpu.SemaphoreType.DMA((steps,)),
+            pltpu.SemaphoreType.DMA((2, steps)),
+            pltpu.SemaphoreType.DMA,
         ],
         compiler_params=pltpu.CompilerParams(vmem_limit_bytes=LEFT_LIMIT),
         cost_estimate=cost(rows, cols, rank),
-    )(matrix, left_t, right)
+    )(*(pltpu.with_memory_space_constraint(a, pltpu.HBM) for a in (matrix, left_t, right)))
 
 
 def right_phase(half, matrix, left_t, right, *source):
@@ -255,9 +280,10 @@
     partner = [(0, 1), (1, 0)]
     own = jnp.reshape(core, (1,)).astype(jnp.int32)
     other = 1 - own
-    left_t, own, other = lax.optimization_barrier((left_t, own, other))
-
-    sent, matrix = left_phase(matrix, left_t, right, n_col)
+    place = jnp.reshape(lax.axis_index("zh"), (1,)).astype(jnp.int32)
+    left_t, own, other, place = lax.optimization_barrier((left_t, own, other, place))
+
+    sent, matrix, left_t, right = left_phase(matrix, left_t, right, n_col)
     got = lax.all_to_all(sent, "x", 0, 0)
     for_partner, kept, new_left_t = right_phase(other, matrix, left_t, right, got)
     there = lax.ppermute(for_partner, "c", partner)
@@ -269,8 +295,10 @@
     pairs = each * (SUB // ROWS_OF)
     message = on_chip(message_kernel, "message", (n_group, pairs + 1, ROWS_OF, LANE), here, there)
     part = jnp.sum(lax.all_to_all(message, ("y", "zl"), 0, 0), axis=0)
-    part = lax.all_to_all(jnp.broadcast_to(part[None], (n_far, *part.shape)), "zh", 0, 0)
-    done = on_chip(finish_kernel, "finish", (n_group, each, SUB, LANE), part)
+    far = [
+        lax.ppermute(part, "zh", [(i, (i + d) % n_far) for i in range(n_far)]) for d in range(1, n_far)
+    ]
+    done = on_chip(finish_kernel, "finish", (n_group, each, SUB, LANE), part, *far, scalar=place)
     mine = lax.all_to_all(done, ("y", "zl"), 0, 0).reshape(bands, strips, SUB, LANE)
     theirs = lax.ppermute(mine, "c", partner)
     is_first = own[0] == 0

time: 95.4 us -> 95.4 us (level)
  blocking collectives: 64.2 us -> 46.5 us
  starting transfers between devices: 16.7 us -> 30.2 us
  waiting for transfers between devices: 1.34 us -> 6.53 us
  local copies, waits for them, and re-layouts: 1.9 us -> 0 us
  Pallas kernels: 9 us -> 10 us
    all_to_all x1 -> x0, blocking collectives: 17.4 us -> none  [local(): lax.all_to_all(jnp.broadcast_to(part[None], (n_far, *part.shape)), 'zh',...]
    ppermute x0 -> x2, starting transfers between devices: none -> 13.5 us  [local(): lax.ppermute(part, 'zh', [(i, (i + d) % n_far) for i in range(n_far)])]
    ppermute x0 -> x2, waiting for transfers between devices: none -> 5.2 us  [local(): lax.ppermute(part, 'zh', [(i, (i + d) % n_far) for i in range(n_far)])]
    unnamed x6 -> x0, local copies, waits for them, and re-layouts: 1.89 us -> none
    pallas_call x1, Pallas kernels: 4.7 us -> 5.67 us  [left_phase(): pl.pallas_call(left_kernel, name='left_phase', out_shape=[jax.ShapeDtypeS...]
  transfers between devices with their start and end apart: 2 -> 4, of which waited for: 1 -> 2; matrix products, arithmetic and copies ran while one was open for 0% -> 0% of each run, Pallas kernels for 2% -> 2%
where the time goes in v5:
time: 95.4 us; the launch traced here: 95.1 us
  blocking collectives  46.5 us (49%)
  starting transfers between devices  30.2 us (32%)
  Pallas kernels  10 us (10%)
  waiting for transfers between devices  6.53 us (7%)
  other arithmetic  1.15 us (1%)
    all_to_all x1, blocking collectives, local(): part = jnp.sum(lax.all_to_all(message, ('y', 'zl'), 0, 0), axis=0)  19.5 us
    all_to_all x1, blocking collectives, local(): lax.all_to_all(done, ('y', 'zl'), 0, 0).reshape(bands, strips, SUB, LANE)  17.4 us
    ppermute x2, starting transfers between devices, local(): lax.ppermute(part, 'zh', [(i, (i + d) % n_far) for i in range(n_far)])  13.5 us
    ppermute x1, starting transfers between devices, local(): there = lax.ppermute(for_partner, 'c', partner)  11.2 us
    all_to_all x1, blocking collectives, local(): got = lax.all_to_all(sent, 'x', 0, 0)  9.55 us
    pallas_call x1, Pallas kernels, left_phase(): pl.pallas_call(left_kernel, name='left_phase', out_shape=[jax.ShapeDtypeS...  5.67 us
    ppermute x1, starting transfers between devices, local(): theirs = lax.ppermute(mine, 'c', partner)  5.47 us
    ppermute x2, waiting for transfers between devices, local(): lax.ppermute(part, 'zh', [(i, (i + d) % n_far) for i in range(n_far)])  5.2 us
  transfers between devices with their start and end apart: 4, of which 2 were waited for; matrix products, arithmetic and copies ran while one was open for 0% of the time, Pallas kernels for 2%

profile of v5, /device:TPU:1, one launch (start us, length us, event | category | flops | bytes accessed | tf_op | source)
XLA Modules:
  0.0 95.1 jit_solution(11732087919360111337)
XLA Ops:
  0.6 5.7 %left_phase.1 = (f32[4,9,8,128]{3,2,1,0:T(8,128)S(1)}, bf16[256,6144]{1,0:T(8,128)(2,1)S(1)}, f32[32,256]{1,0:T(8,128)S(1)}, f32[32,6144]{1,0:T(8,128)S(1)}) custom-call(bf16[256,6144]{1,0:T(8,128)(2,1)} %matrix_hbm.1, f32[32,256]{1,0:T(8,128)} %left_hbm, f32[32,6144]{1,0:T(8,128)} %right_hbm.1), custom_call_target="tpu_custom_call" | custom-call | flops 704643072 | bytes 4718592 | tf_op jit(solution)/shard_map/left_phase/pallas_call | solution.py:236
  6.3 9.5 %all_to_all.15.refs_0_ = f32[4,9,8,128]{3,2,1,0:T(8,128)S(1)} all-to-all(f32[4,9,8,128]{3,2,1,0:T(8,128)S(1)} %get-tuple-element.18), channel_id=1, replica_groups=mesh['y'=8,'zh'=3,'zl'=4,'c'=2,'x'=4] {'x'}, dimensions={0} | all-to-all | bytes 294912 | tf_op jit(solution)/shard_map/all_to_all | solution.py:287
  15.9 2.2 %right_first.1 = (f32[100,8,128]{2,1,0:T(8,128)S(1)}, f32[32,256]{1,0:T(8,128)S(1)}, f32[32,256]{1,0:T(8,128)}) custom-call(s32[1]{0:T(128)S(6)} %sub.3.half_ref, bf16[256,6144]{1,0:T(8,128)(2,1)S(1)} %get-tuple-element.15.matrix_ref, f32[32,256]{1,0:T(8,128)S(1)} %get-tuple-element.16.left_ref, f32[32,6144]{1,0:T(8,128)S(1)} %get-tuple-element.17.right_ref, ...), custom_call_target="tpu_custom_call" | custom-call | flops 352321536 | bytes 2359296 | tf_op jit(solution)/shard_map/right_first/pallas_call | solution.py:264
  18.0 11.2 %collective-permute-start = (f32[100,8,128]{2,1,0:T(8,128)S(1)}, f32[100,8,128]{2,1,0:T(8,128)S(1)}, u32[]{:S(2)}, u32[]{:S(2)}) collective-permute-start(f32[100,8,128]{2,1,0:T(8,128)S(1)} %get-tuple-element.23), channel_id=1, source_target_pairs={{0,4},{4,0},{1,5},{5,1},{2,6},{6,2},{3,7},{7,3},{8,12},{12,8},{9,1... | collective-permute-start | bytes 1228808 | tf_op jit(solution)/shard_map/ppermute | solution.py:289
  29.3 1.9 %right_second.1.here_ref = f32[100,8,128]{2,1,0:T(8,128)S(1)} custom-call(s32[1]{0:T(128)} %bitcast.half_ref, bf16[256,6144]{1,0:T(8,128)(2,1)S(1)} %get-tuple-element.15.matrix_ref, f32[32,256]{1,0:T(8,128)S(1)} %get-tuple-element.22.left_ref, f32[32,6144]{1,0:T(8,128)S(1)} %get-tuple-element.17.right_ref), custom_call_target="tpu_custom_call" | custom-call | flops 352321536 | bytes 2359296 | tf_op jit(solution)/shard_map/right_second/pallas_call | solution.py:264
  31.2 0.0 collective-permute-done.there_ref
  31.2 0.1 message.1
  31.3 19.5 %all_to_all.16 = f32[32,13,2,128]{3,2,1,0:T(2,128)S(1)} all-to-all(f32[32,13,2,128]{3,2,1,0:T(2,128)S(1)} %message.1), channel_id=1, replica_groups=mesh['y'=8,'zh'=3,'zl'=4,'c'=2,'x'=4] {'y','zl'}, dimensions={0} | all-to-all | bytes 851968 | tf_op jit(solution)/shard_map/all_to_all | solution.py:297
  50.8 0.1 reduce_sum.9.refs_0_
  50.9 10.3 %collective-permute-start.1 = (f32[13,2,128]{2,1,0:T(2,128)S(1)}, f32[13,2,128]{2,1,0:T(2,128)S(1)}, u32[]{:S(2)}, u32[]{:S(2)}) collective-permute-start(f32[13,2,128]{2,1,0:T(2,128)S(1)} %reduce_sum.9.refs_0_), channel_id=1, source_target_pairs={{0,32},{32,64},{64,0},{1,33},{33,65},{65,1},{2,34},{34,66},{66,2},... | collective-permute-start | bytes 39944 | tf_op jit(solution)/shard_map/ppermute | solution.py:299
  61.2 3.1 %collective-permute-start.2 = (f32[13,2,128]{2,1,0:T(2,128)S(1)}, f32[13,2,128]{2,1,0:T(2,128)S(1)}, u32[]{:S(2)}, u32[]{:S(2)}) collective-permute-start(f32[13,2,128]{2,1,0:T(2,128)S(1)} %reduce_sum.9.refs_0_), channel_id=1, source_target_pairs={{0,64},{32,0},{64,32},{1,65},{33,1},{65,33},{2,66},{34,2},{66,34},... | collective-permute-start | bytes 39944 | tf_op jit(solution)/shard_map/ppermute | solution.py:299
  64.4 0.0 collective-permute-done.1.refs_1_
  64.4 5.2 %collective-permute-done.2.refs_2_ = f32[13,2,128]{2,1,0:T(2,128)S(1)} collective-permute-done((f32[13,2,128]{2,1,0:T(2,128)S(1)}, f32[13,2,128]{2,1,0:T(2,128)S(1)}, u32[]{:S(2)}, u32[]{:S(2)}) %collective-permute-start.2) | collective-permute-done | bytes 13344 | tf_op jit(solution)/shard_map/ppermute | solution.py:299
  69.6 0.2 finish.1
  69.8 17.4 %all_to_all.17 = f32[32,3,8,128]{3,2,1,0:T(8,128)S(1)} all-to-all(f32[32,3,8,128]{3,2,1,0:T(8,128)S(1)} %finish.1), channel_id=1, replica_groups=mesh['y'=8,'zh'=3,'zl'=4,'c'=2,'x'=4] {'y','zl'}, dimensions={0} | all-to-all | bytes 786432 | tf_op jit(solution)/shard_map/all_to_all | solution.py:302
  87.2 5.5 %collective-permute-start.3 = (f32[4,24,8,128]{3,2,1,0:T(8,128)S(1)}, f32[4,24,8,128]{3,2,1,0:T(8,128)S(1)}, u32[]{:S(2)}, u32[]{:S(2)}) collective-permute-start(f32[4,24,8,128]{3,2,1,0:T(8,128)S(1)} %bitcast.13), channel_id=1, source_target_pairs={{0,4},{4,0},{1,5},{5,1},{2,6},{6,2},{3,7},{7,3},{8,12},{12,8},{9,1... | collective-permute-start | bytes 1179656 | tf_op jit(solution)/shard_map/ppermute | solution.py:303
  92.7 1.3 %collective-permute-done.3 = f32[4,24,8,128]{3,2,1,0:T(8,128)S(1)} collective-permute-done((f32[4,24,8,128]{3,2,1,0:T(8,128)S(1)}, f32[4,24,8,128]{3,2,1,0:T(8,128)S(1)}, u32[]{:S(2)}, u32[]{:S(2)}) %collective-permute-start.3) | collective-permute-done | bytes 393248 | tf_op jit(solution)/shard_map/ppermute | solution.py:303
  94.1 0.1 broadcast_select_fusion.1
  94.1 1.0 %fusion = f32[32,6144]{1,0:T(8,128)} fusion(f32[32,6144]{1,0:T(8,128)S(1)} %get-tuple-element.17.right_ref, f32[4,24,8,128]{3,2,1,0:T(8,128)S(1)} %get-tuple-element.25, f32[4,24,8,128]{3,2,1,0:T(8,128)S(1)} %get-tuple-element.24), kind=kLoop, calls=%fused_computation.1 | loop fusion | flops 393216 | bytes 2359296 | tf_op jit(solution)/shard_map/mul | solution.py:308
Async XLA Ops:
  18.0 13.1 %collective-permute-start = (f32[100,8,128]{2,1,0:T(8,128)S(1)}, f32[100,8,128]{2,1,0:T(8,128)S(1)}, u32[]{:S(2)}, u32[]{:S(2)}) collective-permute-start(f32[100,8,128]{2,1,0:T(8,128)S(1)} %get-tuple-element.23), channel_id=1, source_target_pairs={{0,4},{4,0},{1,5},{5,1},{2,6},{6,2},{3,7},{7,3},{8,12},{12,8},{9,1... | collective-permute-start | bytes 1228808 | tf_op jit(solution)/shard_map/ppermute | solution.py:289
  50.9 13.5 %collective-permute-start.1 = (f32[13,2,128]{2,1,0:T(2,128)S(1)}, f32[13,2,128]{2,1,0:T(2,128)S(1)}, u32[]{:S(2)}, u32[]{:S(2)}) collective-permute-start(f32[13,2,128]{2,1,0:T(2,128)S(1)} %reduce_sum.9.refs_0_), channel_id=1, source_target_pairs={{0,32},{32,64},{64,0},{1,33},{33,65},{65,1},{2,34},{34,66},{66,2},... | collective-permute-start | bytes 39944 | tf_op jit(solution)/shard_map/ppermute | solution.py:299
  61.2 8.4 %collective-permute-start.2 = (f32[13,2,128]{2,1,0:T(2,128)S(1)}, f32[13,2,128]{2,1,0:T(2,128)S(1)}, u32[]{:S(2)}, u32[]{:S(2)}) collective-permute-start(f32[13,2,128]{2,1,0:T(2,128)S(1)} %reduce_sum.9.refs_0_), channel_id=1, source_target_pairs={{0,64},{32,0},{64,32},{1,65},{33,1},{65,33},{2,66},{34,2},{66,34},... | collective-permute-start | bytes 39944 | tf_op jit(solution)/shard_map/ppermute | solution.py:299
  87.2 6.8 %collective-permute-start.3 = (f32[4,24,8,128]{3,2,1,0:T(8,128)S(1)}, f32[4,24,8,128]{3,2,1,0:T(8,128)S(1)}, u32[]{:S(2)}, u32[]{:S(2)}) collective-permute-start(f32[4,24,8,128]{3,2,1,0:T(8,128)S(1)} %bitcast.13), channel_id=1, source_target_pairs={{0,4},{4,0},{1,5},{5,1},{2,6},{6,2},{3,7},{7,3},{8,12},{12,8},{9,1... | collective-permute-start | bytes 1179656 | tf_op jit(solution)/shard_map/ppermute | solution.py:303

commit v6 on v5

--- a/solution.py
+++ b/solution.py
@@ -9,6 +9,7 @@
 
 SUB, LANE = 8, 128
 ROWS_OF = 2
+AHEAD = 2
 F32, BF16 = jnp.float32, jnp.bfloat16
 NT = (((1,), (1,)), ((), ()))
 
@@ -65,7 +66,7 @@
 
     fetch_left = pltpu.make_async_copy(left_hbm, left_ref, left_sem)
     fetch_left.start()
-    for i in range(steps):
+    for i in range(min(AHEAD, steps)):
         for fetch in fetches(i):
             fetch.start()
     both_ref[...] = jnp.zeros_like(both_ref)
@@ -74,6 +75,11 @@
     stacked = stack_left(left_ref[...])
 
     def body(i, summed):
+        @pl.when(i + AHEAD < steps)
+        def _():
+            for fetch in fetches(i + AHEAD):
+                fetch.start()
+
         for fetch in fetches(i):
             fetch.wait()
         highs, lows, q_highs, q_lows = [], [], [], []
@@ -174,24 +180,11 @@
             out_ref[t // each, t % each * per_tile + r] = tile[r * ROWS_OF : (r + 1) * ROWS_OF]
 
 
-def finish_kernel(place_ref, *refs):
-    *parts, out_ref = refs
-    n = len(parts)
-    far_of = [lax.rem(place_ref[0] - source + n, n) for source in range(n)]
-
-    def ordered(i):
-        total = None
-        for far in far_of:
-            value = parts[0][i]
-            for d in range(1, n):
-                value = jnp.where(far == d, parts[d][i], value)
-            total = value if total is None else total + value
-        return total
-
+def finish_kernel(part_ref, out_ref):
     per_tile = SUB // ROWS_OF
-    pairs = parts[0].shape[0] - 1
+    pairs = part_ref.shape[1] - 1
     group = lax.broadcasted_iota(jnp.int32, (ROWS_OF, LANE), 1) // (LANE // per_tile)
-    rows = [ordered(i) for i in range(pairs + 1)]
+    rows = [sum(part_ref[f, i] for f in range(part_ref.shape[0])) for i in range(pairs + 1)]
     mass = jnp.concatenate(
         [jnp.max(jnp.where(group == r, rows[pairs], 0.0), axis=1, keepdims=True) for r in range(per_tile)], axis=0
     )
@@ -201,16 +194,15 @@
             out_ref[p, e] = tile
 
 
-def on_chip(kernel, name, shape, *args, scalar=None):
-    scalars = () if scalar is None else (scalar,)
+def on_chip(kernel, name, shape, *args):
     return pl.pallas_call(
         kernel,
         name=name,
         out_shape=jax.ShapeDtypeStruct(shape, F32),
-        in_specs=[pl.BlockSpec(memory_space=pltpu.SMEM)] * len(scalars) + [ON_CHIP] * len(args),
+        in_specs=[ON_CHIP] * len(args),
         out_specs=ON_CHIP,
         compiler_params=PARAMS,
-    )(*scalars, *args)
+    )(*args)
 
 
 def widths(cols):
@@ -280,8 +272,7 @@
     partner = [(0, 1), (1, 0)]
     own = jnp.reshape(core, (1,)).astype(jnp.int32)
     other = 1 - own
-    place = jnp.reshape(lax.axis_index("zh"), (1,)).astype(jnp.int32)
-    left_t, own, other, place = lax.optimization_barrier((left_t, own, other, place))
+    left_t, own, other = lax.optimization_barrier((left_t, own, other))
 
     sent, matrix, left_t, right = left_phase(matrix, left_t, right, n_col)
     got = lax.all_to_all(sent, "x", 0, 0)
@@ -295,10 +286,8 @@
     pairs = each * (SUB // ROWS_OF)
     message = on_chip(message_kernel, "message", (n_group, pairs + 1, ROWS_OF, LANE), here, there)
     part = jnp.sum(lax.all_to_all(message, ("y", "zl"), 0, 0), axis=0)
-    far = [
-        lax.ppermute(part, "zh", [(i, (i + d) % n_far) for i in range(n_far)]) for d in range(1, n_far)
-    ]
-    done = on_chip(finish_kernel, "finish", (n_group, each, SUB, LANE), part, *far, scalar=place)
+    part = lax.all_to_all(jnp.broadcast_to(part[None], (n_far, *part.shape)), "zh", 0, 0)
+    done = on_chip(finish_kernel, "finish", (n_group, each, SUB, LANE), part)
     mine = lax.all_to_all(done, ("y", "zl"), 0, 0).reshape(bands, strips, SUB, LANE)
     theirs = lax.ppermute(mine, "c", partner)
     is_first = own[0] == 0
@@ -310,7 +299,7 @@
 
 def factor(mesh):
     n_row, n_col = mesh.shape["row"], mesh.shape["col"]
-    n_far, n_near = (3, 4) if n_row % 24 == 0 else (1, 2)
+    n_far, n_near = (6, 2) if n_row % 24 == 0 else (1, 2)
     shape = (n_row // (2 * n_far * n_near), n_far, n_near, 2, n_col)
     return Mesh(mesh.devices.reshape(shape), ("y", "zh", "zl", "c", "x"))
 

time: 95.4 us -> 92.7 us (0.972)
  blocking collectives: 46.5 us -> 61.6 us
  starting transfers between devices: 30.2 us -> 18.4 us
  waiting for transfers between devices: 6.53 us -> 1.33 us
    all_to_all x0 -> x1, blocking collectives: none -> 21.5 us  [local(): lax.all_to_all(jnp.broadcast_to(part[None], (n_far, *part.shape)), 'zh',...]
    ppermute x2 -> x0, starting transfers between devices: 13.5 us -> none  [local(): lax.ppermute(part, 'zh', [(i, (i + d) % n_far) for i in range(n_far)])]
    ppermute x2 -> x0, waiting for transfers between devices: 5.2 us -> none  [local(): lax.ppermute(part, 'zh', [(i, (i + d) % n_far) for i in range(n_far)])]
    all_to_all x1, blocking collectives: 17.4 us -> 14.2 us  [local(): lax.all_to_all(done, ('y', 'zl'), 0, 0).reshape(bands, strips, SUB, LANE)]
    all_to_all x1, blocking collectives: 19.5 us -> 16.3 us  [local(): part = jnp.sum(lax.all_to_all(message, ('y', 'zl'), 0, 0), axis=0)]
    ppermute x1, starting transfers between devices: 5.47 us -> 7.16 us  [local(): theirs = lax.ppermute(mine, 'c', partner)]
  transfers between devices with their start and end apart: 4 -> 2, of which waited for: 2 -> 1; matrix products, arithmetic and copies ran while one was open for 0% -> 0% of each run, Pallas kernels for 2% -> 2%
where the time goes in v6:
time: 92.7 us; the launch traced here: 92.3 us
  blocking collectives  61.6 us (66%)
  starting transfers between devices  18.4 us (20%)
  Pallas kernels  9.19 us (10%)
  waiting for transfers between devices  1.33 us (1%)
  other arithmetic  1.14 us (1%)
    all_to_all x1, blocking collectives, local(): lax.all_to_all(jnp.broadcast_to(part[None], (n_far, *part.shape)), 'zh',...  21.5 us
    all_to_all x1, blocking collectives, local(): part = jnp.sum(lax.all_to_all(message, ('y', 'zl'), 0, 0), axis=0)  16.3 us
    all_to_all x1, blocking collectives, local(): lax.all_to_all(done, ('y', 'zl'), 0, 0).reshape(bands, strips, SUB, LANE)  14.2 us
    ppermute x1, starting transfers between devices, local(): there = lax.ppermute(for_partner, 'c', partner)  11.2 us
    all_to_all x1, blocking collectives, local(): got = lax.all_to_all(sent, 'x', 0, 0)  9.55 us
    ppermute x1, starting transfers between devices, local(): theirs = lax.ppermute(mine, 'c', partner)  7.16 us
    pallas_call x1, Pallas kernels, left_phase(): pl.pallas_call(left_kernel, name='left_phase', out_shape=[jax.ShapeDtypeS...  4.87 us
    pallas_call x2, Pallas kernels, right_phase(): pl.pallas_call(functools.partial(right_kernel, bool(source)), name='right...  4.05 us
  transfers between devices with their start and end apart: 2, of which 1 were waited for; matrix products, arithmetic and copies ran while one was open for 0% of the time, Pallas kernels for 2%

profile of v6, /device:TPU:1, one launch (start us, length us, event | category | flops | bytes accessed | tf_op | source)
XLA Modules:
  0.0 92.3 jit_solution(9900876712216823447)
XLA Ops:
  0.6 4.9 %left_phase.1 = (f32[4,9,8,128]{3,2,1,0:T(8,128)S(1)}, bf16[256,6144]{1,0:T(8,128)(2,1)S(1)}, f32[32,256]{1,0:T(8,128)S(1)}, f32[32,6144]{1,0:T(8,128)S(1)}) custom-call(bf16[256,6144]{1,0:T(8,128)(2,1)} %matrix_hbm.1, f32[32,256]{1,0:T(8,128)} %left_hbm, f32[32,6144]{1,0:T(8,128)} %right_hbm.1), custom_call_target="tpu_custom_call" | custom-call | flops 704643072 | bytes 4718592 | tf_op jit(solution)/shard_map/left_phase/pallas_call | solution.py:228
  5.5 9.5 %all_to_all.20.refs_0_ = f32[4,9,8,128]{3,2,1,0:T(8,128)S(1)} all-to-all(f32[4,9,8,128]{3,2,1,0:T(8,128)S(1)} %get-tuple-element.17), channel_id=1, replica_groups=mesh['y'=8,'zh'=6,'zl'=2,'c'=2,'x'=4] {'x'}, dimensions={0} | all-to-all | bytes 294912 | tf_op jit(solution)/shard_map/all_to_all | solution.py:278
  15.1 2.2 %right_first.1 = (f32[100,8,128]{2,1,0:T(8,128)S(1)}, f32[32,256]{1,0:T(8,128)S(1)}, f32[32,256]{1,0:T(8,128)}) custom-call(s32[1]{0:T(128)S(6)} %sub.3.half_ref, bf16[256,6144]{1,0:T(8,128)(2,1)S(1)} %get-tuple-element.14.matrix_ref, f32[32,256]{1,0:T(8,128)S(1)} %get-tuple-element.15.left_ref, f32[32,6144]{1,0:T(8,128)S(1)} %get-tuple-element.16.right_ref, ...), custom_call_target="tpu_custom_call" | custom-call | flops 352321536 | bytes 2359296 | tf_op jit(solution)/shard_map/right_first/pallas_call | solution.py:256
  17.2 11.2 %collective-permute-start = (f32[100,8,128]{2,1,0:T(8,128)S(1)}, f32[100,8,128]{2,1,0:T(8,128)S(1)}, u32[]{:S(2)}, u32[]{:S(2)}) collective-permute-start(f32[100,8,128]{2,1,0:T(8,128)S(1)} %get-tuple-element.21), channel_id=1, source_target_pairs={{0,4},{4,0},{1,5},{5,1},{2,6},{6,2},{3,7},{7,3},{8,12},{12,8},{9,1... | collective-permute-start | bytes 1228808 | tf_op jit(solution)/shard_map/ppermute | solution.py:280
  28.5 1.9 %right_second.1.here_ref = f32[100,8,128]{2,1,0:T(8,128)S(1)} custom-call(s32[1]{0:T(128)} %bitcast.half_ref, bf16[256,6144]{1,0:T(8,128)(2,1)S(1)} %get-tuple-element.14.matrix_ref, f32[32,256]{1,0:T(8,128)S(1)} %get-tuple-element.20.left_ref, f32[32,6144]{1,0:T(8,128)S(1)} %get-tuple-element.16.right_ref), custom_call_target="tpu_custom_call" | custom-call | flops 352321536 | bytes 2359296 | tf_op jit(solution)/shard_map/right_second/pallas_call | solution.py:256
  30.4 0.0 collective-permute-done.there_ref
  30.4 0.1 message.1
  30.4 16.3 %all_to_all.21 = f32[16,25,2,128]{3,2,1,0:T(2,128)S(1)} all-to-all(f32[16,25,2,128]{3,2,1,0:T(2,128)S(1)} %message.1), channel_id=1, replica_groups=mesh['y'=8,'zh'=6,'zl'=2,'c'=2,'x'=4] {'y','zl'}, dimensions={0} | all-to-all | bytes 819200 | tf_op jit(solution)/shard_map/all_to_all | solution.py:288
  46.7 0.1 reduce_sum.9
  46.9 21.5 %all_to_all.22.part_ref = f32[6,25,2,128]{3,2,1,0:T(2,128)S(1)} all-to-all(f32[6,25,2,128]{3,2,1,0:T(2,128)S(1)} %broadcast_in_dim.2), channel_id=1, replica_groups=mesh['y'=8,'zh'=6,'zl'=2,'c'=2,'x'=4] {'zh'}, dimensions={0} | all-to-all | bytes 307200 | tf_op jit(solution)/shard_map/all_to_all | solution.py:289
  68.4 0.2 finish.1
  68.6 14.2 %all_to_all.23 = f32[16,6,8,128]{3,2,1,0:T(8,128)S(1)} all-to-all(f32[16,6,8,128]{3,2,1,0:T(8,128)S(1)} %finish.1), channel_id=1, replica_groups=mesh['y'=8,'zh'=6,'zl'=2,'c'=2,'x'=4] {'y','zl'}, dimensions={0} | all-to-all | bytes 786432 | tf_op jit(solution)/shard_map/all_to_all | solution.py:291
  82.8 7.2 %collective-permute-start.1 = (f32[4,24,8,128]{3,2,1,0:T(8,128)S(1)}, f32[4,24,8,128]{3,2,1,0:T(8,128)S(1)}, u32[]{:S(2)}, u32[]{:S(2)}) collective-permute-start(f32[4,24,8,128]{3,2,1,0:T(8,128)S(1)} %bitcast.12), channel_id=1, source_target_pairs={{0,4},{4,0},{1,5},{5,1},{2,6},{6,2},{3,7},{7,3},{8,12},{12,8},{9,1... | collective-permute-start | bytes 1179656 | tf_op jit(solution)/shard_map/ppermute | solution.py:292
  90.0 1.3 %collective-permute-done.1 = f32[4,24,8,128]{3,2,1,0:T(8,128)S(1)} collective-permute-done((f32[4,24,8,128]{3,2,1,0:T(8,128)S(1)}, f32[4,24,8,128]{3,2,1,0:T(8,128)S(1)}, u32[]{:S(2)}, u32[]{:S(2)}) %collective-permute-start.1) | collective-permute-done | bytes 393248 | tf_op jit(solution)/shard_map/ppermute | solution.py:292
  91.3 0.1 broadcast_select_fusion.1
  91.4 1.0 %fusion = f32[32,6144]{1,0:T(8,128)} fusion(f32[32,6144]{1,0:T(8,128)S(1)} %get-tuple-element.16.right_ref, f32[4,24,8,128]{3,2,1,0:T(8,128)S(1)} %get-tuple-element.23, f32[4,24,8,128]{3,2,1,0:T(8,128)S(1)} %get-tuple-element.22), kind=kLoop, calls=%fused_computation.1 | loop fusion | flops 393216 | bytes 2359296 | tf_op jit(solution)/shard_map/mul | solution.py:297
  (1 shorter events, 0.0 us)
Async XLA Ops:
  17.2 13.1 %collective-permute-start = (f32[100,8,128]{2,1,0:T(8,128)S(1)}, f32[100,8,128]{2,1,0:T(8,128)S(1)}, u32[]{:S(2)}, u32[]{:S(2)}) collective-permute-start(f32[100,8,128]{2,1,0:T(8,128)S(1)} %get-tuple-element.21), channel_id=1, source_target_pairs={{0,4},{4,0},{1,5},{5,1},{2,6},{6,2},{3,7},{7,3},{8,12},{12,8},{9,1... | collective-permute-start | bytes 1228808 | tf_op jit(solution)/shard_map/ppermute | solution.py:280
  82.8 8.5 %collective-permute-start.1 = (f32[4,24,8,128]{3,2,1,0:T(8,128)S(1)}, f32[4,24,8,128]{3,2,1,0:T(8,128)S(1)}, u32[]{:S(2)}, u32[]{:S(2)}) collective-permute-start(f32[4,24,8,128]{3,2,1,0:T(8,128)S(1)} %bitcast.12), channel_id=1, source_target_pairs={{0,4},{4,0},{1,5},{5,1},{2,6},{6,2},{3,7},{7,3},{8,12},{12,8},{9,1... | collective-permute-start | bytes 1179656 | tf_op jit(solution)/shard_map/ppermute | solution.py:292

commit v7 on v6

--- a/solution.py
+++ b/solution.py
@@ -9,7 +9,7 @@
 
 SUB, LANE = 8, 128
 ROWS_OF = 2
-AHEAD = 2
+LEFT_STEP, RIGHT_STEP = 2048, 3072
 F32, BF16 = jnp.float32, jnp.bfloat16
 NT = (((1,), (1,)), ((), ()))
 
@@ -54,11 +54,11 @@
 def left_kernel(matrix_hbm, left_hbm, right_hbm, out_ref, matrix_ref, left_ref, right_ref, both_ref, rest_ref, sems, left_sem):
     rank, rows = left_ref.shape
     cols = right_ref.shape[1]
-    width, chunk = widths(cols)
-    steps = cols // width
+    width, chunk = widths(cols, LEFT_STEP)
+    steps, piece = cols // width, width // 2
 
     def fetches(i):
-        at = pl.ds(pl.multiple_of(i * width, width), width)
+        at = pl.ds(pl.multiple_of(i * piece, piece), piece)
         return (
             pltpu.make_async_copy(right_hbm.at[:, at], right_ref.at[:, at], sems.at[0, i]),
             pltpu.make_async_copy(matrix_hbm.at[:, at], matrix_ref.at[:, at], sems.at[1, i]),
@@ -66,7 +66,7 @@
 
     fetch_left = pltpu.make_async_copy(left_hbm, left_ref, left_sem)
     fetch_left.start()
-    for i in range(min(AHEAD, steps)):
+    for i in range(2 if steps == 1 else 3):
         for fetch in fetches(i):
             fetch.start()
     both_ref[...] = jnp.zeros_like(both_ref)
@@ -75,15 +75,17 @@
     stacked = stack_left(left_ref[...])
 
     def body(i, summed):
-        @pl.when(i + AHEAD < steps)
-        def _():
-            for fetch in fetches(i + AHEAD):
-                fetch.start()
-
-        for fetch in fetches(i):
-            fetch.wait()
+        for ahead in (3, 4):
+            @pl.when(2 * i + ahead < 2 * steps)
+            def _():
+                for fetch in fetches(2 * i + ahead):
+                    fetch.start()
+
         highs, lows, q_highs, q_lows = [], [], [], []
         for c in range(width // chunk):
+            if c * chunk % piece == 0:
+                for fetch in fetches(2 * i + c * chunk // piece):
+                    fetch.wait()
             at = pl.ds(pl.multiple_of(i * width + c * chunk, chunk), chunk)
             right = right_ref[:, at]
             high, low, (q_high, q_low) = quotient_of(stacked, right, matrix_ref[:, at])
@@ -95,16 +97,15 @@
         high = jnp.concatenate(highs, axis=1)
         low = jnp.concatenate(lows, axis=1)
         both_ref[...] += lax.dot_general(
-            jnp.concatenate(q_highs, axis=1), jnp.concatenate([high, low], axis=0), NT, preferred_element_type=F32
+            jnp.concatenate([high, low], axis=0), jnp.concatenate(q_highs, axis=1), NT, preferred_element_type=F32
         )
         rest_ref[...] += lax.dot_general(
-            jnp.concatenate(q_lows, axis=1), high, NT, preferred_element_type=F32
+            high, jnp.concatenate(q_lows, axis=1), NT, preferred_element_type=F32
         )
         return summed
 
     mass = lax.fori_loop(0, steps, body, jnp.zeros((rank, LANE), F32))
-    both = both_ref[...].T
-    total = both[:rank] + both[rank:] + rest_ref[...].T
+    total = both_ref[:rank] + both_ref[rank:] + rest_ref[...]
     bands, strips = rank // SUB, rows // LANE
     packed = pack_column(jnp.sum(mass, axis=1, keepdims=True))
     for peer in range(out_ref.shape[0]):
@@ -136,7 +137,7 @@
     pair = jnp.concatenate([new_high, new_low], axis=0)
 
     half = right_ref.shape[1] // 2
-    width, chunk = widths(half)
+    width, chunk = widths(half, RIGHT_STEP)
     per_band = half // LANE
     wide = chunk // LANE
     sums = jnp.sum(new, axis=1, keepdims=True)
@@ -205,8 +206,8 @@
     )(*args)
 
 
-def widths(cols):
-    width = 1024 if cols % 1024 == 0 else LANE
+def widths(cols, most):
+    width = next((w for w in (3072, 2048, 1024) if w <= most and cols % w == 0), LANE)
     return width, min(width, 256)
 
 
@@ -223,7 +224,7 @@
 
 def left_phase(matrix, left_t, right, n_col):
     (rank, rows), cols = left_t.shape, right.shape[1]
-    steps = cols // widths(cols)[0]
+    steps = 2 * (cols // widths(cols, LEFT_STEP)[0])
     n_tiles = rank * rows // (SUB * LANE) + 1
     return pl.pallas_call(
         left_kernel,
@@ -237,8 +238,8 @@
         in_specs=[pl.BlockSpec(memory_space=pltpu.HBM)] * 3,
         out_specs=[ON_CHIP] * 4,
         scratch_shapes=[
-            pltpu.VMEM((rows, 2 * rank), F32),
-            pltpu.VMEM((rows, rank), F32),
+            pltpu.VMEM((2 * rank, rows), F32),
+            pltpu.VMEM((rank, rows), F32),
             pltpu.SemaphoreType.DMA((2, steps)),
             pltpu.SemaphoreType.DMA,
         ],

time: 92.7 us -> 91.9 us (level)
    pallas_call x2, Pallas kernels: 4.05 us -> 2.81 us  [right_phase(): pl.pallas_call(functools.partial(right_kernel, bool(source)), name='right...]
  transfers between devices with their start and end apart: 2 -> 2, of which waited for: 1 -> 2; matrix products, arithmetic and copies ran while one was open for 0% -> 0% of each run, Pallas kernels for 2% -> 1%
where the time goes in v7:
time: 91.9 us; the launch traced here: 91.5 us
  blocking collectives  61.6 us (67%)
  starting transfers between devices  18.3 us (20%)
  Pallas kernels  8.32 us (9%)
  waiting for transfers between devices  1.47 us (2%)
  other arithmetic  1.14 us (1%)
    all_to_all x1, blocking collectives, local(): lax.all_to_all(jnp.broadcast_to(part[None], (n_far, *part.shape)), 'zh',...  21.7 us
    all_to_all x1, blocking collectives, local(): part = jnp.sum(lax.all_to_all(message, ('y', 'zl'), 0, 0), axis=0)  15.7 us
    all_to_all x1, blocking collectives, local(): lax.all_to_all(done, ('y', 'zl'), 0, 0).reshape(bands, strips, SUB, LANE)  14.6 us
    ppermute x1, starting transfers between devices, local(): there = lax.ppermute(for_partner, 'c', partner)  11.2 us
    all_to_all x1, blocking collectives, local(): got = lax.all_to_all(sent, 'x', 0, 0)  9.55 us
    ppermute x1, starting transfers between devices, local(): theirs = lax.ppermute(mine, 'c', partner)  7.02 us
    pallas_call x1, Pallas kernels, left_phase(): pl.pallas_call(left_kernel, name='left_phase', out_shape=[jax.ShapeDtypeS...  5.24 us
    pallas_call x2, Pallas kernels, right_phase(): pl.pallas_call(functools.partial(right_kernel, bool(source)), name='right...  2.81 us
  transfers between devices with their start and end apart: 2, of which 2 were waited for; matrix products, arithmetic and copies ran while one was open for 0% of the time, Pallas kernels for 1%

profile of v7, /device:TPU:1, one launch (start us, length us, event | category | flops | bytes accessed | tf_op | source)
XLA Modules:
  0.0 91.5 jit_solution(8766140844868349955)
XLA Ops:
  0.6 5.2 %left_phase.1 = (f32[4,9,8,128]{3,2,1,0:T(8,128)S(1)}, bf16[256,6144]{1,0:T(8,128)(2,1)S(1)}, f32[32,256]{1,0:T(8,128)S(1)}, f32[32,6144]{1,0:T(8,128)S(1)}) custom-call(bf16[256,6144]{1,0:T(8,128)(2,1)} %matrix_hbm.1, f32[32,256]{1,0:T(8,128)} %left_hbm, f32[32,6144]{1,0:T(8,128)} %right_hbm.1), custom_call_target="tpu_custom_call" | custom-call | flops 704643072 | bytes 4718592 | tf_op jit(solution)/shard_map/left_phase/pallas_call | solution.py:229
  5.9 9.5 %all_to_all.20.refs_0_ = f32[4,9,8,128]{3,2,1,0:T(8,128)S(1)} all-to-all(f32[4,9,8,128]{3,2,1,0:T(8,128)S(1)} %get-tuple-element.17), channel_id=1, replica_groups=mesh['y'=8,'zh'=6,'zl'=2,'c'=2,'x'=4] {'x'}, dimensions={0} | all-to-all | bytes 294912 | tf_op jit(solution)/shard_map/all_to_all | solution.py:279
  15.4 1.6 %right_first.1 = (f32[100,8,128]{2,1,0:T(8,128)S(1)}, f32[32,256]{1,0:T(8,128)S(1)}, f32[32,256]{1,0:T(8,128)}) custom-call(s32[1]{0:T(128)S(6)} %sub.3.half_ref, bf16[256,6144]{1,0:T(8,128)(2,1)S(1)} %get-tuple-element.14.matrix_ref, f32[32,256]{1,0:T(8,128)S(1)} %get-tuple-element.15.left_ref, f32[32,6144]{1,0:T(8,128)S(1)} %get-tuple-element.16.right_ref, ...), custom_call_target="tpu_custom_call" | custom-call | flops 352321536 | bytes 2359296 | tf_op jit(solution)/shard_map/right_first/pallas_call | solution.py:257
  17.0 11.2 %collective-permute-start = (f32[100,8,128]{2,1,0:T(8,128)S(1)}, f32[100,8,128]{2,1,0:T(8,128)S(1)}, u32[]{:S(2)}, u32[]{:S(2)}) collective-permute-start(f32[100,8,128]{2,1,0:T(8,128)S(1)} %get-tuple-element.21), channel_id=1, source_target_pairs={{0,4},{4,0},{1,5},{5,1},{2,6},{6,2},{3,7},{7,3},{8,12},{12,8},{9,1... | collective-permute-start | bytes 1228808 | tf_op jit(solution)/shard_map/ppermute | solution.py:281
  28.3 1.2 %right_second.1.here_ref = f32[100,8,128]{2,1,0:T(8,128)S(1)} custom-call(s32[1]{0:T(128)} %bitcast.half_ref, bf16[256,6144]{1,0:T(8,128)(2,1)S(1)} %get-tuple-element.14.matrix_ref, f32[32,256]{1,0:T(8,128)S(1)} %get-tuple-element.20.left_ref, f32[32,6144]{1,0:T(8,128)S(1)} %get-tuple-element.16.right_ref), custom_call_target="tpu_custom_call" | custom-call | flops 352321536 | bytes 2359296 | tf_op jit(solution)/shard_map/right_second/pallas_call | solution.py:257
  29.5 0.1 collective-permute-done.there_ref
  29.6 0.1 message.1
  29.7 15.7 %all_to_all.21 = f32[16,25,2,128]{3,2,1,0:T(2,128)S(1)} all-to-all(f32[16,25,2,128]{3,2,1,0:T(2,128)S(1)} %message.1), channel_id=1, replica_groups=mesh['y'=8,'zh'=6,'zl'=2,'c'=2,'x'=4] {'y','zl'}, dimensions={0} | all-to-all | bytes 819200 | tf_op jit(solution)/shard_map/all_to_all | solution.py:289
  45.4 0.1 reduce_sum.9
  45.6 21.7 %all_to_all.22.part_ref = f32[6,25,2,128]{3,2,1,0:T(2,128)S(1)} all-to-all(f32[6,25,2,128]{3,2,1,0:T(2,128)S(1)} %broadcast_in_dim.2), channel_id=1, replica_groups=mesh['y'=8,'zh'=6,'zl'=2,'c'=2,'x'=4] {'zh'}, dimensions={0} | all-to-all | bytes 307200 | tf_op jit(solution)/shard_map/all_to_all | solution.py:290
  67.3 0.2 finish.1
  67.5 14.6 %all_to_all.23 = f32[16,6,8,128]{3,2,1,0:T(8,128)S(1)} all-to-all(f32[16,6,8,128]{3,2,1,0:T(8,128)S(1)} %finish.1), channel_id=1, replica_groups=mesh['y'=8,'zh'=6,'zl'=2,'c'=2,'x'=4] {'y','zl'}, dimensions={0} | all-to-all | bytes 786432 | tf_op jit(solution)/shard_map/all_to_all | solution.py:292
  82.2 7.0 %collective-permute-start.1 = (f32[4,24,8,128]{3,2,1,0:T(8,128)S(1)}, f32[4,24,8,128]{3,2,1,0:T(8,128)S(1)}, u32[]{:S(2)}, u32[]{:S(2)}) collective-permute-start(f32[4,24,8,128]{3,2,1,0:T(8,128)S(1)} %bitcast.12), channel_id=1, source_target_pairs={{0,4},{4,0},{1,5},{5,1},{2,6},{6,2},{3,7},{7,3},{8,12},{12,8},{9,1... | collective-permute-start | bytes 1179656 | tf_op jit(solution)/shard_map/ppermute | solution.py:293
  89.2 1.3 %collective-permute-done.1 = f32[4,24,8,128]{3,2,1,0:T(8,128)S(1)} collective-permute-done((f32[4,24,8,128]{3,2,1,0:T(8,128)S(1)}, f32[4,24,8,128]{3,2,1,0:T(8,128)S(1)}, u32[]{:S(2)}, u32[]{:S(2)}) %collective-permute-start.1) | collective-permute-done | bytes 393248 | tf_op jit(solution)/shard_map/ppermute | solution.py:293
  90.5 0.1 broadcast_select_fusion.1
  90.6 1.0 %fusion = f32[32,6144]{1,0:T(8,128)} fusion(f32[32,6144]{1,0:T(8,128)S(1)} %get-tuple-element.16.right_ref, f32[4,24,8,128]{3,2,1,0:T(8,128)S(1)} %get-tuple-element.23, f32[4,24,8,128]{3,2,1,0:T(8,128)S(1)} %get-tuple-element.22), kind=kLoop, calls=%fused_computation.1 | loop fusion | flops 393216 | bytes 2359296 | tf_op jit(solution)/shard_map/mul | solution.py:298
  (1 shorter events, 0.0 us)
Async XLA Ops:
  17.0 12.6 %collective-permute-start = (f32[100,8,128]{2,1,0:T(8,128)S(1)}, f32[100,8,128]{2,1,0:T(8,128)S(1)}, u32[]{:S(2)}, u32[]{:S(2)}) collective-permute-start(f32[100,8,128]{2,1,0:T(8,128)S(1)} %get-tuple-element.21), channel_id=1, source_target_pairs={{0,4},{4,0},{1,5},{5,1},{2,6},{6,2},{3,7},{7,3},{8,12},{12,8},{9,1... | collective-permute-start | bytes 1228808 | tf_op jit(solution)/shard_map/ppermute | solution.py:281
  82.2 8.4 %collective-permute-start.1 = (f32[4,24,8,128]{3,2,1,0:T(8,128)S(1)}, f32[4,24,8,128]{3,2,1,0:T(8,128)S(1)}, u32[]{:S(2)}, u32[]{:S(2)}) collective-permute-start(f32[4,24,8,128]{3,2,1,0:T(8,128)S(1)} %bitcast.12), channel_id=1, source_target_pairs={{0,4},{4,0},{1,5},{5,1},{2,6},{6,2},{3,7},{7,3},{8,12},{12,8},{9,1... | collective-permute-start | bytes 1179656 | tf_op jit(solution)/shard_map/ppermute | solution.py:293

commit v8 on v7

--- a/solution.py
+++ b/solution.py
@@ -9,7 +9,7 @@
 
 SUB, LANE = 8, 128
 ROWS_OF = 2
-LEFT_STEP, RIGHT_STEP = 2048, 3072
+LEFT_STEP, RIGHT_STEP = 3072, 3072
 F32, BF16 = jnp.float32, jnp.bfloat16
 NT = (((1,), (1,)), ((), ()))
 
@@ -97,15 +97,16 @@
         high = jnp.concatenate(highs, axis=1)
         low = jnp.concatenate(lows, axis=1)
         both_ref[...] += lax.dot_general(
-            jnp.concatenate([high, low], axis=0), jnp.concatenate(q_highs, axis=1), NT, preferred_element_type=F32
+            jnp.concatenate(q_highs, axis=1), jnp.concatenate([high, low], axis=0), NT, preferred_element_type=F32
         )
         rest_ref[...] += lax.dot_general(
-            high, jnp.concatenate(q_lows, axis=1), NT, preferred_element_type=F32
+            jnp.concatenate(q_lows, axis=1), high, NT, preferred_element_type=F32
         )
         return summed
 
     mass = lax.fori_loop(0, steps, body, jnp.zeros((rank, LANE), F32))
-    total = both_ref[:rank] + both_ref[rank:] + rest_ref[...]
+    both = both_ref[...].T
+    total = both[:rank] + both[rank:] + rest_ref[...].T
     bands, strips = rank // SUB, rows // LANE
     packed = pack_column(jnp.sum(mass, axis=1, keepdims=True))
     for peer in range(out_ref.shape[0]):
@@ -238,8 +239,8 @@
         in_specs=[pl.BlockSpec(memory_space=pltpu.HBM)] * 3,
         out_specs=[ON_CHIP] * 4,
         scratch_shapes=[
-            pltpu.VMEM((2 * rank, rows), F32),
-            pltpu.VMEM((rank, rows), F32),
+            pltpu.VMEM((rows, 2 * rank), F32),
+            pltpu.VMEM((rows, rank), F32),
             pltpu.SemaphoreType.DMA((2, steps)),
             pltpu.SemaphoreType.DMA,
         ],

time: 91.9 us -> 91.9 us (level)
  no operation moved by 1% of the time
where the time goes in v8:
time: 91.9 us; the launch traced here: 91.5 us
  blocking collectives  61.6 us (67%)
  starting transfers between devices  18.3 us (20%)
  Pallas kernels  8.31 us (9%)
  waiting for transfers between devices  1.47 us (2%)
  other arithmetic  1.14 us (1%)
    all_to_all x1, blocking collectives, local(): lax.all_to_all(jnp.broadcast_to(part[None], (n_far, *part.shape)), 'zh',...  21.7 us
    all_to_all x1, blocking collectives, local(): part = jnp.sum(lax.all_to_all(message, ('y', 'zl'), 0, 0), axis=0)  15.7 us
    all_to_all x1, blocking collectives, local(): lax.all_to_all(done, ('y', 'zl'), 0, 0).reshape(bands, strips, SUB, LANE)  14.6 us
    ppermute x1, starting transfers between devices, local(): there = lax.ppermute(for_partner, 'c', partner)  11.2 us
    all_to_all x1, blocking collectives, local(): got = lax.all_to_all(sent, 'x', 0, 0)  9.54 us
    ppermute x1, starting transfers between devices, local(): theirs = lax.ppermute(mine, 'c', partner)  7.02 us
    pallas_call x1, Pallas kernels, left_phase(): pl.pallas_call(left_kernel, name='left_phase', out_shape=[jax.ShapeDtypeS...  5.24 us
    pallas_call x2, Pallas kernels, right_phase(): pl.pallas_call(functools.partial(right_kernel, bool(source)), name='right...  2.81 us
  transfers between devices with their start and end apart: 2, of which 2 were waited for; matrix products, arithmetic and copies ran while one was open for 0% of the time, Pallas kernels for 1%

profile of v8, /device:TPU:1, one launch (start us, length us, event | category | flops | bytes accessed | tf_op | source)
XLA Modules:
  0.0 91.5 jit_solution(15707416545421474449)
XLA Ops:
  0.6 5.2 %left_phase.1 = (f32[4,9,8,128]{3,2,1,0:T(8,128)S(1)}, bf16[256,6144]{1,0:T(8,128)(2,1)S(1)}, f32[32,256]{1,0:T(8,128)S(1)}, f32[32,6144]{1,0:T(8,128)S(1)}) custom-call(bf16[256,6144]{1,0:T(8,128)(2,1)} %matrix_hbm.1, f32[32,256]{1,0:T(8,128)} %left_hbm, f32[32,6144]{1,0:T(8,128)} %right_hbm.1), custom_call_target="tpu_custom_call" | custom-call | flops 704643072 | bytes 4718592 | tf_op jit(solution)/shard_map/left_phase/pallas_call | solution.py:230
  5.9 9.5 %all_to_all.20.refs_0_ = f32[4,9,8,128]{3,2,1,0:T(8,128)S(1)} all-to-all(f32[4,9,8,128]{3,2,1,0:T(8,128)S(1)} %get-tuple-element.17), channel_id=1, replica_groups=mesh['y'=8,'zh'=6,'zl'=2,'c'=2,'x'=4] {'x'}, dimensions={0} | all-to-all | bytes 294912 | tf_op jit(solution)/shard_map/all_to_all | solution.py:280
  15.4 1.6 %right_first.1 = (f32[100,8,128]{2,1,0:T(8,128)S(1)}, f32[32,256]{1,0:T(8,128)S(1)}, f32[32,256]{1,0:T(8,128)}) custom-call(s32[1]{0:T(128)S(6)} %sub.3.half_ref, bf16[256,6144]{1,0:T(8,128)(2,1)S(1)} %get-tuple-element.14.matrix_ref, f32[32,256]{1,0:T(8,128)S(1)} %get-tuple-element.15.left_ref, f32[32,6144]{1,0:T(8,128)S(1)} %get-tuple-element.16.right_ref, ...), custom_call_target="tpu_custom_call" | custom-call | flops 352321536 | bytes 2359296 | tf_op jit(solution)/shard_map/right_first/pallas_call | solution.py:258
  17.0 11.2 %collective-permute-start = (f32[100,8,128]{2,1,0:T(8,128)S(1)}, f32[100,8,128]{2,1,0:T(8,128)S(1)}, u32[]{:S(2)}, u32[]{:S(2)}) collective-permute-start(f32[100,8,128]{2,1,0:T(8,128)S(1)} %get-tuple-element.21), channel_id=1, source_target_pairs={{0,4},{4,0},{1,5},{5,1},{2,6},{6,2},{3,7},{7,3},{8,12},{12,8},{9,1... | collective-permute-start | bytes 1228808 | tf_op jit(solution)/shard_map/ppermute | solution.py:282
  28.3 1.2 %right_second.1.here_ref = f32[100,8,128]{2,1,0:T(8,128)S(1)} custom-call(s32[1]{0:T(128)} %bitcast.half_ref, bf16[256,6144]{1,0:T(8,128)(2,1)S(1)} %get-tuple-element.14.matrix_ref, f32[32,256]{1,0:T(8,128)S(1)} %get-tuple-element.20.left_ref, f32[32,6144]{1,0:T(8,128)S(1)} %get-tuple-element.16.right_ref), custom_call_target="tpu_custom_call" | custom-call | flops 352321536 | bytes 2359296 | tf_op jit(solution)/shard_map/right_second/pallas_call | solution.py:258
  29.5 0.1 collective-permute-done.there_ref
  29.6 0.1 message.1
  29.7 15.7 %all_to_all.21 = f32[16,25,2,128]{3,2,1,0:T(2,128)S(1)} all-to-all(f32[16,25,2,128]{3,2,1,0:T(2,128)S(1)} %message.1), channel_id=1, replica_groups=mesh['y'=8,'zh'=6,'zl'=2,'c'=2,'x'=4] {'y','zl'}, dimensions={0} | all-to-all | bytes 819200 | tf_op jit(solution)/shard_map/all_to_all | solution.py:290
  45.4 0.1 reduce_sum.9
  45.6 21.7 %all_to_all.22.part_ref = f32[6,25,2,128]{3,2,1,0:T(2,128)S(1)} all-to-all(f32[6,25,2,128]{3,2,1,0:T(2,128)S(1)} %broadcast_in_dim.2), channel_id=1, replica_groups=mesh['y'=8,'zh'=6,'zl'=2,'c'=2,'x'=4] {'zh'}, dimensions={0} | all-to-all | bytes 307200 | tf_op jit(solution)/shard_map/all_to_all | solution.py:291
  67.3 0.2 finish.1
  67.5 14.6 %all_to_all.23 = f32[16,6,8,128]{3,2,1,0:T(8,128)S(1)} all-to-all(f32[16,6,8,128]{3,2,1,0:T(8,128)S(1)} %finish.1), channel_id=1, replica_groups=mesh['y'=8,'zh'=6,'zl'=2,'c'=2,'x'=4] {'y','zl'}, dimensions={0} | all-to-all | bytes 786432 | tf_op jit(solution)/shard_map/all_to_all | solution.py:293
  82.2 7.0 %collective-permute-start.1 = (f32[4,24,8,128]{3,2,1,0:T(8,128)S(1)}, f32[4,24,8,128]{3,2,1,0:T(8,128)S(1)}, u32[]{:S(2)}, u32[]{:S(2)}) collective-permute-start(f32[4,24,8,128]{3,2,1,0:T(8,128)S(1)} %bitcast.12), channel_id=1, source_target_pairs={{0,4},{4,0},{1,5},{5,1},{2,6},{6,2},{3,7},{7,3},{8,12},{12,8},{9,1... | collective-permute-start | bytes 1179656 | tf_op jit(solution)/shard_map/ppermute | solution.py:294
  89.2 1.3 %collective-permute-done.1 = f32[4,24,8,128]{3,2,1,0:T(8,128)S(1)} collective-permute-done((f32[4,24,8,128]{3,2,1,0:T(8,128)S(1)}, f32[4,24,8,128]{3,2,1,0:T(8,128)S(1)}, u32[]{:S(2)}, u32[]{:S(2)}) %collective-permute-start.1) | collective-permute-done | bytes 393248 | tf_op jit(solution)/shard_map/ppermute | solution.py:294
  90.5 0.1 broadcast_select_fusion.1
  90.6 1.0 %fusion = f32[32,6144]{1,0:T(8,128)} fusion(f32[32,6144]{1,0:T(8,128)S(1)} %get-tuple-element.16.right_ref, f32[4,24,8,128]{3,2,1,0:T(8,128)S(1)} %get-tuple-element.23, f32[4,24,8,128]{3,2,1,0:T(8,128)S(1)} %get-tuple-element.22), kind=kLoop, calls=%fused_computation.1 | loop fusion | flops 393216 | bytes 2359296 | tf_op jit(solution)/shard_map/mul | solution.py:299
  (1 shorter events, 0.0 us)
Async XLA Ops:
  17.0 12.6 %collective-permute-start = (f32[100,8,128]{2,1,0:T(8,128)S(1)}, f32[100,8,128]{2,1,0:T(8,128)S(1)}, u32[]{:S(2)}, u32[]{:S(2)}) collective-permute-start(f32[100,8,128]{2,1,0:T(8,128)S(1)} %get-tuple-element.21), channel_id=1, source_target_pairs={{0,4},{4,0},{1,5},{5,1},{2,6},{6,2},{3,7},{7,3},{8,12},{12,8},{9,1... | collective-permute-start | bytes 1228808 | tf_op jit(solution)/shard_map/ppermute | solution.py:282
  82.2 8.4 %collective-permute-start.1 = (f32[4,24,8,128]{3,2,1,0:T(8,128)S(1)}, f32[4,24,8,128]{3,2,1,0:T(8,128)S(1)}, u32[]{:S(2)}, u32[]{:S(2)}) collective-permute-start(f32[4,24,8,128]{3,2,1,0:T(8,128)S(1)} %bitcast.12), channel_id=1, source_target_pairs={{0,4},{4,0},{1,5},{5,1},{2,6},{6,2},{3,7},{7,3},{8,12},{12,8},{9,1... | collective-permute-start | bytes 1179656 | tf_op jit(solution)/shard_map/ppermute | solution.py:294
